TPU v7x, 32 devices: a whole 2x2x4 slice. The times are simulated.
32 devices in a mesh: lon: 8 (over y, x, core), lat: 4 (over z).
Axes of the slice: x: 2, y: 2, z: 4, core: 2. Of those that a mesh axis runs over, the one named last changes fastest.
Arguments:
- state: float32 [3, 4, 256, 1024], P(None, None, 'lat', 'lon'), may hold values from -0.010253906 to 0.010253906
- depth: float32 [256, 1024], P('lat', 'lon'), may hold values from 0.1 to 1
- source_mask: int32 [8, 32], P('lat', 'lon'), may hold values 0 or 1
- gauge_lat: int32 [4], replicated, may hold values from 0 to 255
- gauge_lon: int32 [4], replicated, may hold values from 0 to 1023
- misfit: float32 [6, 4], replicated, may hold values from -4 to 4
Outputs:
- adjoint_state: float32 [3, 4, 256, 1024], P(None, None, 'lat', 'lon')
- coefficients: float32 [4, 512, 512], P(None, 'lon', 'lat')
All inputs are finite; a program needn't handle non-finite values. No bound on the sum of `source_mask` on one device may be relied on, other than what follows from the above.
Results may differ from a plain program's by a relative error of at most 0.0003.
Values sent between devices are 32-bit elements; how exact they have to be, the bound alone decides.
A program may use at most 64 MiB of HBM per device.

v0:
```python
import math

import jax
import jax.numpy as jnp
from jax import lax
from jax.sharding import PartitionSpec as P

STEPS = 6
KX = 512
KY = 512


time_step = 0.5


def padded_2(block, sides, width):
    for axis, dim in sides:
        count = lax.axis_size(axis)
        forward = [(i, i + 1) for i in range(count - 1)]
        backward = [(target, source) for source, target in forward]
        low = lax.ppermute(
            lax.slice_in_dim(block, block.shape[dim] - width, None, axis=dim), axis, forward
        )
        high = lax.ppermute(lax.slice_in_dim(block, 0, width, axis=dim), axis, backward)
        block = jnp.concatenate([low, block, high], axis=dim)
    return block


def centred_x(f):
    return 0.5 * (f[..., 1:-1, 2:] - f[..., 1:-1, :-2])


def centred_y(f):
    return 0.5 * (f[..., 2:, 1:-1] - f[..., :-2, 1:-1])


def basis(total, modes, start, count):
    cells = start + jnp.arange(count, dtype=jnp.int32)
    order = jnp.arange(modes, dtype=jnp.int32)
    half = modes // 2
    wave = jnp.where(order < half, order, order - half + 1)
    phase = (cells[:, None] * wave[None, :] % total).astype(jnp.float32) * (2.0 * math.pi / total)
    return jnp.where(order[None, :] < half, jnp.cos(phase), jnp.sin(phase))


def gauge_table(gauge_lat, gauge_lon, row_start, col_start, rows, cols):
    row_cells = row_start + jnp.arange(rows, dtype=jnp.int32)
    col_cells = col_start + jnp.arange(cols, dtype=jnp.int32)
    hits = (row_cells[None, :, None] == gauge_lat[:, None, None]) & (
        col_cells[None, None, :] == gauge_lon[:, None, None]
    )
    return hits.astype(jnp.float32)


def on_device(state, depth, source_mask, gauge_lat, gauge_lon, misfit):
    rows, cols = depth.shape
    lat_count = lax.axis_size("lat")
    lon_count = lax.axis_size("lon")
    row_start = lax.axis_index("lat") * rows
    col_start = lax.axis_index("lon") * cols
    total_rows = rows * lat_count
    total_cols = cols * lon_count
    heights, east, north = (state[0], state[1], state[2])
    gauges = gauge_table(gauge_lat, gauge_lon, row_start, col_start, rows, cols)
    for step in range(STEPS):
        rim = padded_2(jnp.stack([east, north]), (("lon", 3), ("lat", 2)), 1)
        heights = (
            heights
            + time_step * (centred_x(rim[0]) + centred_y(rim[1]))
            + gauges * misfit[step][:, None, None]
        )
        padded = padded_2(heights, (("lon", 2), ("lat", 1)), 1)
        east = east + time_step * depth * centred_x(padded)
        north = north + time_step * depth * centred_y(padded)
    fields = jnp.stack([heights, east, north])
    tiles_y, tiles_x = source_mask.shape
    side = rows // tiles_y
    full_mask = (
        jnp.broadcast_to(source_mask[:, None, :, None], (tiles_y, side, tiles_x, side))
        .reshape(rows, cols)
        .astype(jnp.float32)
    )
    masked = heights * full_mask
    lat_basis = basis(total_rows, KY, row_start, rows)
    lon_basis = basis(total_cols, KX, col_start, cols)
    scale = 2.0 / math.sqrt(total_rows * total_cols)
    part = lat_basis
    by_lat = lax.psum_scatter(
        jnp.einsum("yk,ayx->kax", part, masked, precision=lax.Precision.HIGHEST),
        "lat",
        scatter_dimension=0,
        tiled=True,
    )
    part = lon_basis
    owned = lax.psum_scatter(
        jnp.einsum("xk,jax->kaj", part, by_lat, precision=lax.Precision.HIGHEST),
        "lon",
        scatter_dimension=0,
        tiled=True,
    )
    modes = jnp.transpose(owned, (1, 0, 2)) * scale
    return (fields, modes)


def solution(mesh):
    placed = (P(None, None, "lat", "lon"), P("lat", "lon"), P("lat", "lon"), P(), P(), P())
    return jax.shard_map(
        on_device,
        mesh=mesh,
        in_specs=placed,
        out_specs=(P(None, None, "lat", "lon"), P(None, "lon", "lat")),
        check_vma=False,
    )
```

profile of v0, /device:TPU:0, one launch (start us, length us, event | category | flops | bytes accessed | tf_op | source)
XLA Modules:
  0.0 324.6 jit_solution(15201911172647704818)
XLA Ops:
  8.4 1.3 collective-permute-start.1
  9.7 3.0 collective-permute-start
  14.4 1.3 collective-permute-start.3
  15.7 5.6 %collective-permute-start.2 = (f32[2,4,1,130]{3,2,1,0:T(1,128)S(1)}, f32[2,4,1,130]{3,2,1,0:T(1,128)S(1)}, u32[]{:S(2)}, u32[]{:S(2)}) collective-permute-start(f32[2,4,1,130]{3,2,1,0:T(1,128)S(1)} %get-tuple-element.24), channel_id=1, source_target_pairs={{0,1},{1,2},{2,3},{4,5},{5,6},{6,7},{8,9},{9,10},{10,11},{12,13},{... | collective-permute-start | bytes 12488 | tf_op jit(solution)/shard_map/ppermute | solution.py:21
  23.2 4.2 %collective-permute-start.5 = (f32[4,64,1]{2,1,0:T(8,128)S(1)}, f32[4,64,1]{2,1,0:T(8,128)S(1)}, u32[]{:S(2)}, u32[]{:S(2)}) collective-permute-start(f32[4,64,1]{2,1,0:T(8,128)S(1)} %get-tuple-element.82), channel_id=1, source_target_pairs={{0,4},{4,8},{8,12},{12,16},{16,20},{20,24},{24,28},{1,5},{5,9},{9,... | collective-permute-start | bytes 3080 | tf_op jit(solution)/shard_map/ppermute | solution.py:21
  27.4 1.3 collective-permute-start.4
  28.7 5.0 %collective-permute-done.4 = f32[4,64,1]{2,1,0:T(8,128)S(1)} collective-permute-done((f32[4,64,1]{2,1,0:T(8,128)S(1)}, f32[4,64,1]{2,1,0:T(8,128)S(1)}, u32[]{:S(2)}, u32[]{:S(2)}) %collective-permute-start.4) | collective-permute-done | bytes 1056 | tf_op jit(solution)/shard_map/ppermute | solution.py:24
  33.9 4.2 %collective-permute-start.7 = (f32[4,1,130]{2,1,0:T(1,128)S(1)}, f32[4,1,130]{2,1,0:T(1,128)S(1)}, u32[]{:S(2)}, u32[]{:S(2)}) collective-permute-start(f32[4,1,130]{2,1,0:T(1,128)S(1)} %get-tuple-element.59), channel_id=1, source_target_pairs={{0,1},{1,2},{2,3},{4,5},{5,6},{6,7},{8,9},{9,10},{10,11},{12,13},{... | collective-permute-start | bytes 6248 | tf_op jit(solution)/shard_map/ppermute | solution.py:21
  38.1 1.3 collective-permute-start.6
  39.4 4.2 %collective-permute-done.6 = f32[4,1,130]{2,1,0:T(1,128)S(1)} collective-permute-done((f32[4,1,130]{2,1,0:T(1,128)S(1)}, f32[4,1,130]{2,1,0:T(1,128)S(1)}, u32[]{:S(2)}, u32[]{:S(2)}) %collective-permute-start.6) | collective-permute-done | bytes 2112 | tf_op jit(solution)/shard_map/ppermute | solution.py:24
  44.0 1.3 collective-permute-start.9
  45.3 5.1 %collective-permute-start.8 = (f32[2,4,64,1]{3,2,1,0:T(8,128)S(1)}, f32[2,4,64,1]{3,2,1,0:T(8,128)S(1)}, u32[]{:S(2)}, u32[]{:S(2)}) collective-permute-start(f32[2,4,64,1]{3,2,1,0:T(8,128)S(1)} %get-tuple-element.70), channel_id=1, source_target_pairs={{0,4},{4,8},{8,12},{12,16},{16,20},{20,24},{24,28},{1,5},{5,9},{9,... | collective-permute-start | bytes 6152 | tf_op jit(solution)/shard_map/ppermute | solution.py:21
  51.6 1.3 collective-permute-start.11
  52.9 4.5 %collective-permute-start.10 = (f32[2,4,1,130]{3,2,1,0:T(1,128)S(1)}, f32[2,4,1,130]{3,2,1,0:T(1,128)S(1)}, u32[]{:S(2)}, u32[]{:S(2)}) collective-permute-start(f32[2,4,1,130]{3,2,1,0:T(1,128)S(1)} %get-tuple-element.22), channel_id=1, source_target_pairs={{0,1},{1,2},{2,3},{4,5},{5,6},{6,7},{8,9},{9,10},{10,11},{12,13},{... | collective-permute-start | bytes 12488 | tf_op jit(solution)/shard_map/ppermute | solution.py:21
  57.4 1.3 collective-permute-done.10
  59.5 4.7 %collective-permute-start.13 = (f32[4,64,1]{2,1,0:T(8,128)S(1)}, f32[4,64,1]{2,1,0:T(8,128)S(1)}, u32[]{:S(2)}, u32[]{:S(2)}) collective-permute-start(f32[4,64,1]{2,1,0:T(8,128)S(1)} %get-tuple-element.80), channel_id=1, source_target_pairs={{0,4},{4,8},{8,12},{12,16},{16,20},{20,24},{24,28},{1,5},{5,9},{9,... | collective-permute-start | bytes 3080 | tf_op jit(solution)/shard_map/ppermute | solution.py:21
  64.1 1.3 collective-permute-start.12
  65.4 5.0 %collective-permute-done.12 = f32[4,64,1]{2,1,0:T(8,128)S(1)} collective-permute-done((f32[4,64,1]{2,1,0:T(8,128)S(1)}, f32[4,64,1]{2,1,0:T(8,128)S(1)}, u32[]{:S(2)}, u32[]{:S(2)}) %collective-permute-start.12) | collective-permute-done | bytes 1056 | tf_op jit(solution)/shard_map/ppermute | solution.py:24
  70.6 4.2 %collective-permute-start.15 = (f32[4,1,130]{2,1,0:T(1,128)S(1)}, f32[4,1,130]{2,1,0:T(1,128)S(1)}, u32[]{:S(2)}, u32[]{:S(2)}) collective-permute-start(f32[4,1,130]{2,1,0:T(1,128)S(1)} %get-tuple-element.57), channel_id=1, source_target_pairs={{0,1},{1,2},{2,3},{4,5},{5,6},{6,7},{8,9},{9,10},{10,11},{12,13},{... | collective-permute-start | bytes 6248 | tf_op jit(solution)/shard_map/ppermute | solution.py:21
  74.8 1.3 collective-permute-start.14
  76.1 4.2 %collective-permute-done.14 = f32[4,1,130]{2,1,0:T(1,128)S(1)} collective-permute-done((f32[4,1,130]{2,1,0:T(1,128)S(1)}, f32[4,1,130]{2,1,0:T(1,128)S(1)}, u32[]{:S(2)}, u32[]{:S(2)}) %collective-permute-start.14) | collective-permute-done | bytes 2112 | tf_op jit(solution)/shard_map/ppermute | solution.py:24
  80.7 1.3 collective-permute-start.17
  82.0 5.6 %collective-permute-start.16 = (f32[2,4,64,1]{3,2,1,0:T(8,128)S(1)}, f32[2,4,64,1]{3,2,1,0:T(8,128)S(1)}, u32[]{:S(2)}, u32[]{:S(2)}) collective-permute-start(f32[2,4,64,1]{3,2,1,0:T(8,128)S(1)} %get-tuple-element.68), channel_id=1, source_target_pairs={{0,4},{4,8},{8,12},{12,16},{16,20},{20,24},{24,28},{1,5},{5,9},{9,... | collective-permute-start | bytes 6152 | tf_op jit(solution)/shard_map/ppermute | solution.py:21
  88.8 1.3 collective-permute-start.19
  90.1 4.5 %collective-permute-start.18 = (f32[2,4,1,130]{3,2,1,0:T(1,128)S(1)}, f32[2,4,1,130]{3,2,1,0:T(1,128)S(1)}, u32[]{:S(2)}, u32[]{:S(2)}) collective-permute-start(f32[2,4,1,130]{3,2,1,0:T(1,128)S(1)} %get-tuple-element.20), channel_id=1, source_target_pairs={{0,1},{1,2},{2,3},{4,5},{5,6},{6,7},{8,9},{9,10},{10,11},{12,13},{... | collective-permute-start | bytes 12488 | tf_op jit(solution)/shard_map/ppermute | solution.py:21
  94.7 1.3 collective-permute-done.18
  96.7 5.5 %collective-permute-start.21 = (f32[4,64,1]{2,1,0:T(8,128)S(1)}, f32[4,64,1]{2,1,0:T(8,128)S(1)}, u32[]{:S(2)}, u32[]{:S(2)}) collective-permute-start(f32[4,64,1]{2,1,0:T(8,128)S(1)} %get-tuple-element.78), channel_id=1, source_target_pairs={{0,4},{4,8},{8,12},{12,16},{16,20},{20,24},{24,28},{1,5},{5,9},{9,... | collective-permute-start | bytes 3080 | tf_op jit(solution)/shard_map/ppermute | solution.py:21
  102.2 1.3 collective-permute-start.20
  103.5 5.0 %collective-permute-done.20 = f32[4,64,1]{2,1,0:T(8,128)S(1)} collective-permute-done((f32[4,64,1]{2,1,0:T(8,128)S(1)}, f32[4,64,1]{2,1,0:T(8,128)S(1)}, u32[]{:S(2)}, u32[]{:S(2)}) %collective-permute-start.20) | collective-permute-done | bytes 1056 | tf_op jit(solution)/shard_map/ppermute | solution.py:24
  108.7 4.2 %collective-permute-start.23 = (f32[4,1,130]{2,1,0:T(1,128)S(1)}, f32[4,1,130]{2,1,0:T(1,128)S(1)}, u32[]{:S(2)}, u32[]{:S(2)}) collective-permute-start(f32[4,1,130]{2,1,0:T(1,128)S(1)} %get-tuple-element.55), channel_id=1, source_target_pairs={{0,1},{1,2},{2,3},{4,5},{5,6},{6,7},{8,9},{9,10},{10,11},{12,13},{... | collective-permute-start | bytes 6248 | tf_op jit(solution)/shard_map/ppermute | solution.py:21
  112.9 1.3 collective-permute-start.22
  114.2 4.2 %collective-permute-done.22 = f32[4,1,130]{2,1,0:T(1,128)S(1)} collective-permute-done((f32[4,1,130]{2,1,0:T(1,128)S(1)}, f32[4,1,130]{2,1,0:T(1,128)S(1)}, u32[]{:S(2)}, u32[]{:S(2)}) %collective-permute-start.22) | collective-permute-done | bytes 2112 | tf_op jit(solution)/shard_map/ppermute | solution.py:24
  118.8 1.3 collective-permute-start.25
  120.1 6.8 %collective-permute-start.24 = (f32[2,4,64,1]{3,2,1,0:T(8,128)S(1)}, f32[2,4,64,1]{3,2,1,0:T(8,128)S(1)}, u32[]{:S(2)}, u32[]{:S(2)}) collective-permute-start(f32[2,4,64,1]{3,2,1,0:T(8,128)S(1)} %get-tuple-element.66), channel_id=1, source_target_pairs={{0,4},{4,8},{8,12},{12,16},{16,20},{20,24},{24,28},{1,5},{5,9},{9,... | collective-permute-start | bytes 6152 | tf_op jit(solution)/shard_map/ppermute | solution.py:21
  128.1 1.3 collective-permute-start.27
  129.4 4.5 %collective-permute-start.26 = (f32[2,4,1,130]{3,2,1,0:T(1,128)S(1)}, f32[2,4,1,130]{3,2,1,0:T(1,128)S(1)}, u32[]{:S(2)}, u32[]{:S(2)}) collective-permute-start(f32[2,4,1,130]{3,2,1,0:T(1,128)S(1)} %get-tuple-element.18), channel_id=1, source_target_pairs={{0,1},{1,2},{2,3},{4,5},{5,6},{6,7},{8,9},{9,10},{10,11},{12,13},{... | collective-permute-start | bytes 12488 | tf_op jit(solution)/shard_map/ppermute | solution.py:21
  134.0 1.3 collective-permute-done.26
  136.0 5.2 %collective-permute-start.29 = (f32[4,64,1]{2,1,0:T(8,128)S(1)}, f32[4,64,1]{2,1,0:T(8,128)S(1)}, u32[]{:S(2)}, u32[]{:S(2)}) collective-permute-start(f32[4,64,1]{2,1,0:T(8,128)S(1)} %get-tuple-element.76), channel_id=1, source_target_pairs={{0,4},{4,8},{8,12},{12,16},{16,20},{20,24},{24,28},{1,5},{5,9},{9,... | collective-permute-start | bytes 3080 | tf_op jit(solution)/shard_map/ppermute | solution.py:21
  141.2 1.3 collective-permute-start.28
  142.6 5.0 %collective-permute-done.28 = f32[4,64,1]{2,1,0:T(8,128)S(1)} collective-permute-done((f32[4,64,1]{2,1,0:T(8,128)S(1)}, f32[4,64,1]{2,1,0:T(8,128)S(1)}, u32[]{:S(2)}, u32[]{:S(2)}) %collective-permute-start.28) | collective-permute-done | bytes 1056 | tf_op jit(solution)/shard_map/ppermute | solution.py:24
  147.7 4.2 %collective-permute-start.31 = (f32[4,1,130]{2,1,0:T(1,128)S(1)}, f32[4,1,130]{2,1,0:T(1,128)S(1)}, u32[]{:S(2)}, u32[]{:S(2)}) collective-permute-start(f32[4,1,130]{2,1,0:T(1,128)S(1)} %get-tuple-element.53), channel_id=1, source_target_pairs={{0,1},{1,2},{2,3},{4,5},{5,6},{6,7},{8,9},{9,10},{10,11},{12,13},{... | collective-permute-start | bytes 6248 | tf_op jit(solution)/shard_map/ppermute | solution.py:21
  151.9 1.3 collective-permute-start.30
  153.2 4.2 %collective-permute-done.30 = f32[4,1,130]{2,1,0:T(1,128)S(1)} collective-permute-done((f32[4,1,130]{2,1,0:T(1,128)S(1)}, f32[4,1,130]{2,1,0:T(1,128)S(1)}, u32[]{:S(2)}, u32[]{:S(2)}) %collective-permute-start.30) | collective-permute-done | bytes 2112 | tf_op jit(solution)/shard_map/ppermute | solution.py:24
  157.8 1.3 collective-permute-start.33
  159.1 6.8 %collective-permute-start.32 = (f32[2,4,64,1]{3,2,1,0:T(8,128)S(1)}, f32[2,4,64,1]{3,2,1,0:T(8,128)S(1)}, u32[]{:S(2)}, u32[]{:S(2)}) collective-permute-start(f32[2,4,64,1]{3,2,1,0:T(8,128)S(1)} %get-tuple-element.64), channel_id=1, source_target_pairs={{0,4},{4,8},{8,12},{12,16},{16,20},{20,24},{24,28},{1,5},{5,9},{9,... | collective-permute-start | bytes 6152 | tf_op jit(solution)/shard_map/ppermute | solution.py:21
  167.1 1.3 collective-permute-start.35
  168.4 4.5 %collective-permute-start.34 = (f32[2,4,1,130]{3,2,1,0:T(1,128)S(1)}, f32[2,4,1,130]{3,2,1,0:T(1,128)S(1)}, u32[]{:S(2)}, u32[]{:S(2)}) collective-permute-start(f32[2,4,1,130]{3,2,1,0:T(1,128)S(1)} %get-tuple-element.16), channel_id=1, source_target_pairs={{0,1},{1,2},{2,3},{4,5},{5,6},{6,7},{8,9},{9,10},{10,11},{12,13},{... | collective-permute-start | bytes 12488 | tf_op jit(solution)/shard_map/ppermute | solution.py:21
  173.0 1.3 collective-permute-done.34
  175.0 5.2 %collective-permute-start.37 = (f32[4,64,1]{2,1,0:T(8,128)S(1)}, f32[4,64,1]{2,1,0:T(8,128)S(1)}, u32[]{:S(2)}, u32[]{:S(2)}) collective-permute-start(f32[4,64,1]{2,1,0:T(8,128)S(1)} %get-tuple-element.74), channel_id=1, source_target_pairs={{0,4},{4,8},{8,12},{12,16},{16,20},{20,24},{24,28},{1,5},{5,9},{9,... | collective-permute-start | bytes 3080 | tf_op jit(solution)/shard_map/ppermute | solution.py:21
  180.2 1.3 collective-permute-start.36
  181.6 5.0 %collective-permute-done.36 = f32[4,64,1]{2,1,0:T(8,128)S(1)} collective-permute-done((f32[4,64,1]{2,1,0:T(8,128)S(1)}, f32[4,64,1]{2,1,0:T(8,128)S(1)}, u32[]{:S(2)}, u32[]{:S(2)}) %collective-permute-start.36) | collective-permute-done | bytes 1056 | tf_op jit(solution)/shard_map/ppermute | solution.py:24
  186.7 4.2 %collective-permute-start.39 = (f32[4,1,130]{2,1,0:T(1,128)S(1)}, f32[4,1,130]{2,1,0:T(1,128)S(1)}, u32[]{:S(2)}, u32[]{:S(2)}) collective-permute-start(f32[4,1,130]{2,1,0:T(1,128)S(1)} %get-tuple-element.51), channel_id=1, source_target_pairs={{0,1},{1,2},{2,3},{4,5},{5,6},{6,7},{8,9},{9,10},{10,11},{12,13},{... | collective-permute-start | bytes 6248 | tf_op jit(solution)/shard_map/ppermute | solution.py:21
  192.2 4.2 %collective-permute-done.38 = f32[4,1,130]{2,1,0:T(1,128)S(1)} collective-permute-done((f32[4,1,130]{2,1,0:T(1,128)S(1)}, f32[4,1,130]{2,1,0:T(1,128)S(1)}, u32[]{:S(2)}, u32[]{:S(2)}) %collective-permute-start.38) | collective-permute-done | bytes 2112 | tf_op jit(solution)/shard_map/ppermute | solution.py:24
  198.1 6.8 %collective-permute-start.40 = (f32[2,4,64,1]{3,2,1,0:T(8,128)S(1)}, f32[2,4,64,1]{3,2,1,0:T(8,128)S(1)}, u32[]{:S(2)}, u32[]{:S(2)}) collective-permute-start(f32[2,4,64,1]{3,2,1,0:T(8,128)S(1)} %get-tuple-element.62), channel_id=1, source_target_pairs={{0,4},{4,8},{8,12},{12,16},{16,20},{20,24},{24,28},{1,5},{5,9},{9,... | collective-permute-start | bytes 6152 | tf_op jit(solution)/shard_map/ppermute | solution.py:21
  207.5 4.5 %collective-permute-start.42 = (f32[2,4,1,130]{3,2,1,0:T(1,128)S(1)}, f32[2,4,1,130]{3,2,1,0:T(1,128)S(1)}, u32[]{:S(2)}, u32[]{:S(2)}) collective-permute-start(f32[2,4,1,130]{3,2,1,0:T(1,128)S(1)} %get-tuple-element.14), channel_id=1, source_target_pairs={{0,1},{1,2},{2,3},{4,5},{5,6},{6,7},{8,9},{9,10},{10,11},{12,13},{... | collective-permute-start | bytes 12488 | tf_op jit(solution)/shard_map/ppermute | solution.py:21
  213.9 2.6 fusion.77
  216.7 38.4 %reduce-scatter.2.cloned.1.call-done = f32[128,4,128]{2,0,1:T(8,128)} async-done(((f32[512,4,128]{2,0,1:T(8,128)}), f32[128,4,128]{2,0,1:T(8,128)}) %reduce-scatter.2.cloned.1.call-update) | async-done | bytes 262160 | tf_op jit(solution)/shard_map/reduce_scatter | solution.py:88
  255.1 3.0 convolution_bitcast_fusion
  258.1 1.3 copy.9
  259.6 1.6 collective-permute-start.45
  262.5 3.3 %collective-permute-done.44 = f32[4,64,1]{2,1,0:T(8,128)S(1)} collective-permute-done((f32[4,64,1]{2,1,0:T(8,128)S(1)}, f32[4,64,1]{2,1,0:T(8,128)S(1)}, u32[]{:S(2)}, u32[]{:S(2)}) %collective-permute-start.44) | collective-permute-done | bytes 1056 | tf_op jit(solution)/shard_map/ppermute | solution.py:24
  265.9 1.3 collective-permute-start.47
  270.5 2.5 collective-permute-done.46
  274.0 42.2 %all-reduce.3.cloned.1.call-done = f32[512,4,128]{2,1,0:T(4,128)} async-done(((f32[512,4,128]{2,1,0:T(4,128)}), f32[512,4,128]{2,1,0:T(4,128)}) %all-reduce.3.cloned.1.call-update) | async-done | bytes 1048592
  (119 shorter events, 28.5 us)
Async XLA Ops:
  7.2 7.0 %copy-start = (f32[3,4,64,128]{3,2,1,0:T(8,128)S(1)}, f32[3,4,64,128]{3,2,1,0:T(8,128)}, u32[]{:S(2)}) copy-start(f32[3,4,64,128]{3,2,1,0:T(8,128)} %param.6) | copy-start | bytes 1179652
  7.2 247.9 %reduce-scatter.2.cloned.1.call-start = ((), (), s32[]{:S(2)}) async-start(), calls=%async_computation.1 | async-start | bytes 1310720 | tf_op jit(solution)/shard_map/reduce_scatter | solution.py:88
  8.4 5.8 %collective-permute-start.1 = (f32[2,4,64,1]{3,2,1,0:T(8,128)S(1)}, f32[2,4,64,1]{3,2,1,0:T(8,128)S(1)}, u32[]{:S(2)}, u32[]{:S(2)}) collective-permute-start(f32[2,4,64,1]{3,2,1,0:T(8,128)S(1)} %get-tuple-element.61), channel_id=1, source_target_pairs={{4,0},{8,4},{12,8},{16,12},{20,16},{24,20},{28,24},{5,1},{9,5},{13... | collective-permute-start | bytes 6152 | tf_op jit(solution)/shard_map/ppermute | solution.py:24
  9.7 4.5 %collective-permute-start = (f32[2,4,64,1]{3,2,1,0:T(8,128)S(1)}, f32[2,4,64,1]{3,2,1,0:T(8,128)S(1)}, u32[]{:S(2)}, u32[]{:S(2)}) collective-permute-start(f32[2,4,64,1]{3,2,1,0:T(8,128)S(1)} %get-tuple-element.60), channel_id=1, source_target_pairs={{0,4},{4,8},{8,12},{12,16},{16,20},{20,24},{24,28},{1,5},{5,9},{9,... | collective-permute-start | bytes 6152 | tf_op jit(solution)/shard_map/ppermute | solution.py:21
  12.8 0.7 copy-start.4
  13.5 0.7 copy-start.5
  14.4 6.9 %copy-start.1 = (f32[6,4]{0,1:T(4,128)S(1)}, f32[6,4]{0,1:T(4,128)}, u32[]{:S(2)}) copy-start(f32[6,4]{0,1:T(4,128)} %param.11) | copy-start | bytes 292
  14.4 7.1 %collective-permute-start.3 = (f32[2,4,1,130]{3,2,1,0:T(1,128)S(1)}, f32[2,4,1,130]{3,2,1,0:T(1,128)S(1)}, u32[]{:S(2)}, u32[]{:S(2)}) collective-permute-start(f32[2,4,1,130]{3,2,1,0:T(1,128)S(1)} %get-tuple-element.25), channel_id=1, source_target_pairs={{1,0},{2,1},{3,2},{5,4},{6,5},{7,6},{9,8},{10,9},{11,10},{13,12},{... | collective-permute-start | bytes 12488 | tf_op jit(solution)/shard_map/ppermute | solution.py:24
  15.7 6.9 %collective-permute-start.2 = (f32[2,4,1,130]{3,2,1,0:T(1,128)S(1)}, f32[2,4,1,130]{3,2,1,0:T(1,128)S(1)}, u32[]{:S(2)}, u32[]{:S(2)}) collective-permute-start(f32[2,4,1,130]{3,2,1,0:T(1,128)S(1)} %get-tuple-element.24), channel_id=1, source_target_pairs={{0,1},{1,2},{2,3},{4,5},{5,6},{6,7},{8,9},{9,10},{10,11},{12,13},{... | collective-permute-start | bytes 12488 | tf_op jit(solution)/shard_map/ppermute | solution.py:21
  23.2 5.5 %collective-permute-start.5 = (f32[4,64,1]{2,1,0:T(8,128)S(1)}, f32[4,64,1]{2,1,0:T(8,128)S(1)}, u32[]{:S(2)}, u32[]{:S(2)}) collective-permute-start(f32[4,64,1]{2,1,0:T(8,128)S(1)} %get-tuple-element.82), channel_id=1, source_target_pairs={{0,4},{4,8},{8,12},{12,16},{16,20},{20,24},{24,28},{1,5},{5,9},{9,... | collective-permute-start | bytes 3080 | tf_op jit(solution)/shard_map/ppermute | solution.py:21
  27.4 12.0 %copy-start.2 = (f32[64,128]{1,0:T(8,128)S(1)}, f32[64,128]{1,0:T(8,128)}, u32[]{:S(2)}) copy-start(f32[64,128]{1,0:T(8,128)} %param.7) | copy-start | bytes 98308
  27.4 6.4 %collective-permute-start.4 = (f32[4,64,1]{2,1,0:T(8,128)S(1)}, f32[4,64,1]{2,1,0:T(8,128)S(1)}, u32[]{:S(2)}, u32[]{:S(2)}) collective-permute-start(f32[4,64,1]{2,1,0:T(8,128)S(1)} %get-tuple-element.83), channel_id=1, source_target_pairs={{4,0},{8,4},{12,8},{16,12},{20,16},{24,20},{28,24},{5,1},{9,5},{13... | collective-permute-start | bytes 3080 | tf_op jit(solution)/shard_map/ppermute | solution.py:24
  33.9 5.5 %collective-permute-start.7 = (f32[4,1,130]{2,1,0:T(1,128)S(1)}, f32[4,1,130]{2,1,0:T(1,128)S(1)}, u32[]{:S(2)}, u32[]{:S(2)}) collective-permute-start(f32[4,1,130]{2,1,0:T(1,128)S(1)} %get-tuple-element.59), channel_id=1, source_target_pairs={{0,1},{1,2},{2,3},{4,5},{5,6},{6,7},{8,9},{9,10},{10,11},{12,13},{... | collective-permute-start | bytes 6248 | tf_op jit(solution)/shard_map/ppermute | solution.py:21
  38.1 5.5 %collective-permute-start.6 = (f32[4,1,130]{2,1,0:T(1,128)S(1)}, f32[4,1,130]{2,1,0:T(1,128)S(1)}, u32[]{:S(2)}, u32[]{:S(2)}) collective-permute-start(f32[4,1,130]{2,1,0:T(1,128)S(1)} %get-tuple-element.58), channel_id=1, source_target_pairs={{1,0},{2,1},{3,2},{5,4},{6,5},{7,6},{9,8},{10,9},{11,10},{13,12},{... | collective-permute-start | bytes 6248 | tf_op jit(solution)/shard_map/ppermute | solution.py:24
  44.0 6.4 %collective-permute-start.9 = (f32[2,4,64,1]{3,2,1,0:T(8,128)S(1)}, f32[2,4,64,1]{3,2,1,0:T(8,128)S(1)}, u32[]{:S(2)}, u32[]{:S(2)}) collective-permute-start(f32[2,4,64,1]{3,2,1,0:T(8,128)S(1)} %get-tuple-element.71), channel_id=1, source_target_pairs={{4,0},{8,4},{12,8},{16,12},{20,16},{24,20},{28,24},{5,1},{9,5},{13... | collective-permute-start | bytes 6152 | tf_op jit(solution)/shard_map/ppermute | solution.py:24
  45.3 6.2 %collective-permute-start.8 = (f32[2,4,64,1]{3,2,1,0:T(8,128)S(1)}, f32[2,4,64,1]{3,2,1,0:T(8,128)S(1)}, u32[]{:S(2)}, u32[]{:S(2)}) collective-permute-start(f32[2,4,64,1]{3,2,1,0:T(8,128)S(1)} %get-tuple-element.70), channel_id=1, source_target_pairs={{0,4},{4,8},{8,12},{12,16},{16,20},{20,24},{24,28},{1,5},{5,9},{9,... | collective-permute-start | bytes 6152 | tf_op jit(solution)/shard_map/ppermute | solution.py:21
  51.6 5.9 %collective-permute-start.11 = (f32[2,4,1,130]{3,2,1,0:T(1,128)S(1)}, f32[2,4,1,130]{3,2,1,0:T(1,128)S(1)}, u32[]{:S(2)}, u32[]{:S(2)}) collective-permute-start(f32[2,4,1,130]{3,2,1,0:T(1,128)S(1)} %get-tuple-element.23), channel_id=1, source_target_pairs={{1,0},{2,1},{3,2},{5,4},{6,5},{7,6},{9,8},{10,9},{11,10},{13,12},{... | collective-permute-start | bytes 12488 | tf_op jit(solution)/shard_map/ppermute | solution.py:24
  52.9 5.9 %collective-permute-start.10 = (f32[2,4,1,130]{3,2,1,0:T(1,128)S(1)}, f32[2,4,1,130]{3,2,1,0:T(1,128)S(1)}, u32[]{:S(2)}, u32[]{:S(2)}) collective-permute-start(f32[2,4,1,130]{3,2,1,0:T(1,128)S(1)} %get-tuple-element.22), channel_id=1, source_target_pairs={{0,1},{1,2},{2,3},{4,5},{5,6},{6,7},{8,9},{9,10},{10,11},{12,13},{... | collective-permute-start | bytes 12488 | tf_op jit(solution)/shard_map/ppermute | solution.py:21
  59.5 6.0 %collective-permute-start.13 = (f32[4,64,1]{2,1,0:T(8,128)S(1)}, f32[4,64,1]{2,1,0:T(8,128)S(1)}, u32[]{:S(2)}, u32[]{:S(2)}) collective-permute-start(f32[4,64,1]{2,1,0:T(8,128)S(1)} %get-tuple-element.80), channel_id=1, source_target_pairs={{0,4},{4,8},{8,12},{12,16},{16,20},{20,24},{24,28},{1,5},{5,9},{9,... | collective-permute-start | bytes 3080 | tf_op jit(solution)/shard_map/ppermute | solution.py:21
  64.1 6.4 %collective-permute-start.12 = (f32[4,64,1]{2,1,0:T(8,128)S(1)}, f32[4,64,1]{2,1,0:T(8,128)S(1)}, u32[]{:S(2)}, u32[]{:S(2)}) collective-permute-start(f32[4,64,1]{2,1,0:T(8,128)S(1)} %get-tuple-element.81), channel_id=1, source_target_pairs={{4,0},{8,4},{12,8},{16,12},{20,16},{24,20},{28,24},{5,1},{9,5},{13... | collective-permute-start | bytes 3080 | tf_op jit(solution)/shard_map/ppermute | solution.py:24
  70.6 5.5 %collective-permute-start.15 = (f32[4,1,130]{2,1,0:T(1,128)S(1)}, f32[4,1,130]{2,1,0:T(1,128)S(1)}, u32[]{:S(2)}, u32[]{:S(2)}) collective-permute-start(f32[4,1,130]{2,1,0:T(1,128)S(1)} %get-tuple-element.57), channel_id=1, source_target_pairs={{0,1},{1,2},{2,3},{4,5},{5,6},{6,7},{8,9},{9,10},{10,11},{12,13},{... | collective-permute-start | bytes 6248 | tf_op jit(solution)/shard_map/ppermute | solution.py:21
  74.8 5.5 %collective-permute-start.14 = (f32[4,1,130]{2,1,0:T(1,128)S(1)}, f32[4,1,130]{2,1,0:T(1,128)S(1)}, u32[]{:S(2)}, u32[]{:S(2)}) collective-permute-start(f32[4,1,130]{2,1,0:T(1,128)S(1)} %get-tuple-element.56), channel_id=1, source_target_pairs={{1,0},{2,1},{3,2},{5,4},{6,5},{7,6},{9,8},{10,9},{11,10},{13,12},{... | collective-permute-start | bytes 6248 | tf_op jit(solution)/shard_map/ppermute | solution.py:24
  80.7 6.9 %collective-permute-start.17 = (f32[2,4,64,1]{3,2,1,0:T(8,128)S(1)}, f32[2,4,64,1]{3,2,1,0:T(8,128)S(1)}, u32[]{:S(2)}, u32[]{:S(2)}) collective-permute-start(f32[2,4,64,1]{3,2,1,0:T(8,128)S(1)} %get-tuple-element.69), channel_id=1, source_target_pairs={{4,0},{8,4},{12,8},{16,12},{20,16},{24,20},{28,24},{5,1},{9,5},{13... | collective-permute-start | bytes 6152 | tf_op jit(solution)/shard_map/ppermute | solution.py:24
  82.0 6.8 %collective-permute-start.16 = (f32[2,4,64,1]{3,2,1,0:T(8,128)S(1)}, f32[2,4,64,1]{3,2,1,0:T(8,128)S(1)}, u32[]{:S(2)}, u32[]{:S(2)}) collective-permute-start(f32[2,4,64,1]{3,2,1,0:T(8,128)S(1)} %get-tuple-element.68), channel_id=1, source_target_pairs={{0,4},{4,8},{8,12},{12,16},{16,20},{20,24},{24,28},{1,5},{5,9},{9,... | collective-permute-start | bytes 6152 | tf_op jit(solution)/shard_map/ppermute | solution.py:21
  88.8 5.9 %collective-permute-start.19 = (f32[2,4,1,130]{3,2,1,0:T(1,128)S(1)}, f32[2,4,1,130]{3,2,1,0:T(1,128)S(1)}, u32[]{:S(2)}, u32[]{:S(2)}) collective-permute-start(f32[2,4,1,130]{3,2,1,0:T(1,128)S(1)} %get-tuple-element.21), channel_id=1, source_target_pairs={{1,0},{2,1},{3,2},{5,4},{6,5},{7,6},{9,8},{10,9},{11,10},{13,12},{... | collective-permute-start | bytes 12488 | tf_op jit(solution)/shard_map/ppermute | solution.py:24
  90.1 5.9 %collective-permute-start.18 = (f32[2,4,1,130]{3,2,1,0:T(1,128)S(1)}, f32[2,4,1,130]{3,2,1,0:T(1,128)S(1)}, u32[]{:S(2)}, u32[]{:S(2)}) collective-permute-start(f32[2,4,1,130]{3,2,1,0:T(1,128)S(1)} %get-tuple-element.20), channel_id=1, source_target_pairs={{0,1},{1,2},{2,3},{4,5},{5,6},{6,7},{8,9},{9,10},{10,11},{12,13},{... | collective-permute-start | bytes 12488 | tf_op jit(solution)/shard_map/ppermute | solution.py:21
  96.7 6.8 %collective-permute-start.21 = (f32[4,64,1]{2,1,0:T(8,128)S(1)}, f32[4,64,1]{2,1,0:T(8,128)S(1)}, u32[]{:S(2)}, u32[]{:S(2)}) collective-permute-start(f32[4,64,1]{2,1,0:T(8,128)S(1)} %get-tuple-element.78), channel_id=1, source_target_pairs={{0,4},{4,8},{8,12},{12,16},{16,20},{20,24},{24,28},{1,5},{5,9},{9,... | collective-permute-start | bytes 3080 | tf_op jit(solution)/shard_map/ppermute | solution.py:21
  102.2 6.4 %collective-permute-start.20 = (f32[4,64,1]{2,1,0:T(8,128)S(1)}, f32[4,64,1]{2,1,0:T(8,128)S(1)}, u32[]{:S(2)}, u32[]{:S(2)}) collective-permute-start(f32[4,64,1]{2,1,0:T(8,128)S(1)} %get-tuple-element.79), channel_id=1, source_target_pairs={{4,0},{8,4},{12,8},{16,12},{20,16},{24,20},{28,24},{5,1},{9,5},{13... | collective-permute-start | bytes 3080 | tf_op jit(solution)/shard_map/ppermute | solution.py:24
  108.7 5.5 %collective-permute-start.23 = (f32[4,1,130]{2,1,0:T(1,128)S(1)}, f32[4,1,130]{2,1,0:T(1,128)S(1)}, u32[]{:S(2)}, u32[]{:S(2)}) collective-permute-start(f32[4,1,130]{2,1,0:T(1,128)S(1)} %get-tuple-element.55), channel_id=1, source_target_pairs={{0,1},{1,2},{2,3},{4,5},{5,6},{6,7},{8,9},{9,10},{10,11},{12,13},{... | collective-permute-start | bytes 6248 | tf_op jit(solution)/shard_map/ppermute | solution.py:21
  112.9 5.5 %collective-permute-start.22 = (f32[4,1,130]{2,1,0:T(1,128)S(1)}, f32[4,1,130]{2,1,0:T(1,128)S(1)}, u32[]{:S(2)}, u32[]{:S(2)}) collective-permute-start(f32[4,1,130]{2,1,0:T(1,128)S(1)} %get-tuple-element.54), channel_id=1, source_target_pairs={{1,0},{2,1},{3,2},{5,4},{6,5},{7,6},{9,8},{10,9},{11,10},{13,12},{... | collective-permute-start | bytes 6248 | tf_op jit(solution)/shard_map/ppermute | solution.py:24
  118.8 8.1 %collective-permute-start.25 = (f32[2,4,64,1]{3,2,1,0:T(8,128)S(1)}, f32[2,4,64,1]{3,2,1,0:T(8,128)S(1)}, u32[]{:S(2)}, u32[]{:S(2)}) collective-permute-start(f32[2,4,64,1]{3,2,1,0:T(8,128)S(1)} %get-tuple-element.67), channel_id=1, source_target_pairs={{4,0},{8,4},{12,8},{16,12},{20,16},{24,20},{28,24},{5,1},{9,5},{13... | collective-permute-start | bytes 6152 | tf_op jit(solution)/shard_map/ppermute | solution.py:24
  120.1 7.9 %collective-permute-start.24 = (f32[2,4,64,1]{3,2,1,0:T(8,128)S(1)}, f32[2,4,64,1]{3,2,1,0:T(8,128)S(1)}, u32[]{:S(2)}, u32[]{:S(2)}) collective-permute-start(f32[2,4,64,1]{3,2,1,0:T(8,128)S(1)} %get-tuple-element.66), channel_id=1, source_target_pairs={{0,4},{4,8},{8,12},{12,16},{16,20},{20,24},{24,28},{1,5},{5,9},{9,... | collective-permute-start | bytes 6152 | tf_op jit(solution)/shard_map/ppermute | solution.py:21
  128.1 5.9 %collective-permute-start.27 = (f32[2,4,1,130]{3,2,1,0:T(1,128)S(1)}, f32[2,4,1,130]{3,2,1,0:T(1,128)S(1)}, u32[]{:S(2)}, u32[]{:S(2)}) collective-permute-start(f32[2,4,1,130]{3,2,1,0:T(1,128)S(1)} %get-tuple-element.19), channel_id=1, source_target_pairs={{1,0},{2,1},{3,2},{5,4},{6,5},{7,6},{9,8},{10,9},{11,10},{13,12},{... | collective-permute-start | bytes 12488 | tf_op jit(solution)/shard_map/ppermute | solution.py:24
  129.4 5.9 %collective-permute-start.26 = (f32[2,4,1,130]{3,2,1,0:T(1,128)S(1)}, f32[2,4,1,130]{3,2,1,0:T(1,128)S(1)}, u32[]{:S(2)}, u32[]{:S(2)}) collective-permute-start(f32[2,4,1,130]{3,2,1,0:T(1,128)S(1)} %get-tuple-element.18), channel_id=1, source_target_pairs={{0,1},{1,2},{2,3},{4,5},{5,6},{6,7},{8,9},{9,10},{10,11},{12,13},{... | collective-permute-start | bytes 12488 | tf_op jit(solution)/shard_map/ppermute | solution.py:21
  136.0 6.5 %collective-permute-start.29 = (f32[4,64,1]{2,1,0:T(8,128)S(1)}, f32[4,64,1]{2,1,0:T(8,128)S(1)}, u32[]{:S(2)}, u32[]{:S(2)}) collective-permute-start(f32[4,64,1]{2,1,0:T(8,128)S(1)} %get-tuple-element.76), channel_id=1, source_target_pairs={{0,4},{4,8},{8,12},{12,16},{16,20},{20,24},{24,28},{1,5},{5,9},{9,... | collective-permute-start | bytes 3080 | tf_op jit(solution)/shard_map/ppermute | solution.py:21
  141.2 6.4 %collective-permute-start.28 = (f32[4,64,1]{2,1,0:T(8,128)S(1)}, f32[4,64,1]{2,1,0:T(8,128)S(1)}, u32[]{:S(2)}, u32[]{:S(2)}) collective-permute-start(f32[4,64,1]{2,1,0:T(8,128)S(1)} %get-tuple-element.77), channel_id=1, source_target_pairs={{4,0},{8,4},{12,8},{16,12},{20,16},{24,20},{28,24},{5,1},{9,5},{13... | collective-permute-start | bytes 3080 | tf_op jit(solution)/shard_map/ppermute | solution.py:24
  147.7 5.5 %collective-permute-start.31 = (f32[4,1,130]{2,1,0:T(1,128)S(1)}, f32[4,1,130]{2,1,0:T(1,128)S(1)}, u32[]{:S(2)}, u32[]{:S(2)}) collective-permute-start(f32[4,1,130]{2,1,0:T(1,128)S(1)} %get-tuple-element.53), channel_id=1, source_target_pairs={{0,1},{1,2},{2,3},{4,5},{5,6},{6,7},{8,9},{9,10},{10,11},{12,13},{... | collective-permute-start | bytes 6248 | tf_op jit(solution)/shard_map/ppermute | solution.py:21
  151.9 5.5 %collective-permute-start.30 = (f32[4,1,130]{2,1,0:T(1,128)S(1)}, f32[4,1,130]{2,1,0:T(1,128)S(1)}, u32[]{:S(2)}, u32[]{:S(2)}) collective-permute-start(f32[4,1,130]{2,1,0:T(1,128)S(1)} %get-tuple-element.52), channel_id=1, source_target_pairs={{1,0},{2,1},{3,2},{5,4},{6,5},{7,6},{9,8},{10,9},{11,10},{13,12},{... | collective-permute-start | bytes 6248 | tf_op jit(solution)/shard_map/ppermute | solution.py:24
  157.8 8.1 %collective-permute-start.33 = (f32[2,4,64,1]{3,2,1,0:T(8,128)S(1)}, f32[2,4,64,1]{3,2,1,0:T(8,128)S(1)}, u32[]{:S(2)}, u32[]{:S(2)}) collective-permute-start(f32[2,4,64,1]{3,2,1,0:T(8,128)S(1)} %get-tuple-element.65), channel_id=1, source_target_pairs={{4,0},{8,4},{12,8},{16,12},{20,16},{24,20},{28,24},{5,1},{9,5},{13... | collective-permute-start | bytes 6152 | tf_op jit(solution)/shard_map/ppermute | solution.py:24
  159.1 7.9 %collective-permute-start.32 = (f32[2,4,64,1]{3,2,1,0:T(8,128)S(1)}, f32[2,4,64,1]{3,2,1,0:T(8,128)S(1)}, u32[]{:S(2)}, u32[]{:S(2)}) collective-permute-start(f32[2,4,64,1]{3,2,1,0:T(8,128)S(1)} %get-tuple-element.64), channel_id=1, source_target_pairs={{0,4},{4,8},{8,12},{12,16},{16,20},{20,24},{24,28},{1,5},{5,9},{9,... | collective-permute-start | bytes 6152 | tf_op jit(solution)/shard_map/ppermute | solution.py:21
  167.1 5.9 %collective-permute-start.35 = (f32[2,4,1,130]{3,2,1,0:T(1,128)S(1)}, f32[2,4,1,130]{3,2,1,0:T(1,128)S(1)}, u32[]{:S(2)}, u32[]{:S(2)}) collective-permute-start(f32[2,4,1,130]{3,2,1,0:T(1,128)S(1)} %get-tuple-element.17), channel_id=1, source_target_pairs={{1,0},{2,1},{3,2},{5,4},{6,5},{7,6},{9,8},{10,9},{11,10},{13,12},{... | collective-permute-start | bytes 12488 | tf_op jit(solution)/shard_map/ppermute | solution.py:24
  168.4 5.9 %collective-permute-start.34 = (f32[2,4,1,130]{3,2,1,0:T(1,128)S(1)}, f32[2,4,1,130]{3,2,1,0:T(1,128)S(1)}, u32[]{:S(2)}, u32[]{:S(2)}) collective-permute-start(f32[2,4,1,130]{3,2,1,0:T(1,128)S(1)} %get-tuple-element.16), channel_id=1, source_target_pairs={{0,1},{1,2},{2,3},{4,5},{5,6},{6,7},{8,9},{9,10},{10,11},{12,13},{... | collective-permute-start | bytes 12488 | tf_op jit(solution)/shard_map/ppermute | solution.py:21
  175.0 6.5 %collective-permute-start.37 = (f32[4,64,1]{2,1,0:T(8,128)S(1)}, f32[4,64,1]{2,1,0:T(8,128)S(1)}, u32[]{:S(2)}, u32[]{:S(2)}) collective-permute-start(f32[4,64,1]{2,1,0:T(8,128)S(1)} %get-tuple-element.74), channel_id=1, source_target_pairs={{0,4},{4,8},{8,12},{12,16},{16,20},{20,24},{24,28},{1,5},{5,9},{9,... | collective-permute-start | bytes 3080 | tf_op jit(solution)/shard_map/ppermute | solution.py:21
  180.2 6.4 %collective-permute-start.36 = (f32[4,64,1]{2,1,0:T(8,128)S(1)}, f32[4,64,1]{2,1,0:T(8,128)S(1)}, u32[]{:S(2)}, u32[]{:S(2)}) collective-permute-start(f32[4,64,1]{2,1,0:T(8,128)S(1)} %get-tuple-element.75), channel_id=1, source_target_pairs={{4,0},{8,4},{12,8},{16,12},{20,16},{24,20},{28,24},{5,1},{9,5},{13... | collective-permute-start | bytes 3080 | tf_op jit(solution)/shard_map/ppermute | solution.py:24
  186.7 5.5 %collective-permute-start.39 = (f32[4,1,130]{2,1,0:T(1,128)S(1)}, f32[4,1,130]{2,1,0:T(1,128)S(1)}, u32[]{:S(2)}, u32[]{:S(2)}) collective-permute-start(f32[4,1,130]{2,1,0:T(1,128)S(1)} %get-tuple-element.51), channel_id=1, source_target_pairs={{0,1},{1,2},{2,3},{4,5},{5,6},{6,7},{8,9},{9,10},{10,11},{12,13},{... | collective-permute-start | bytes 6248 | tf_op jit(solution)/shard_map/ppermute | solution.py:21
  190.9 5.5 %collective-permute-start.38 = (f32[4,1,130]{2,1,0:T(1,128)S(1)}, f32[4,1,130]{2,1,0:T(1,128)S(1)}, u32[]{:S(2)}, u32[]{:S(2)}) collective-permute-start(f32[4,1,130]{2,1,0:T(1,128)S(1)} %get-tuple-element.50), channel_id=1, source_target_pairs={{1,0},{2,1},{3,2},{5,4},{6,5},{7,6},{9,8},{10,9},{11,10},{13,12},{... | collective-permute-start | bytes 6248 | tf_op jit(solution)/shard_map/ppermute | solution.py:24
  196.8 8.1 %collective-permute-start.41 = (f32[2,4,64,1]{3,2,1,0:T(8,128)S(1)}, f32[2,4,64,1]{3,2,1,0:T(8,128)S(1)}, u32[]{:S(2)}, u32[]{:S(2)}) collective-permute-start(f32[2,4,64,1]{3,2,1,0:T(8,128)S(1)} %get-tuple-element.63), channel_id=1, source_target_pairs={{4,0},{8,4},{12,8},{16,12},{20,16},{24,20},{28,24},{5,1},{9,5},{13... | collective-permute-start | bytes 6152 | tf_op jit(solution)/shard_map/ppermute | solution.py:24
  198.1 7.9 %collective-permute-start.40 = (f32[2,4,64,1]{3,2,1,0:T(8,128)S(1)}, f32[2,4,64,1]{3,2,1,0:T(8,128)S(1)}, u32[]{:S(2)}, u32[]{:S(2)}) collective-permute-start(f32[2,4,64,1]{3,2,1,0:T(8,128)S(1)} %get-tuple-element.62), channel_id=1, source_target_pairs={{0,4},{4,8},{8,12},{12,16},{16,20},{20,24},{24,28},{1,5},{5,9},{9,... | collective-permute-start | bytes 6152 | tf_op jit(solution)/shard_map/ppermute | solution.py:21
  206.1 6.1 %collective-permute-start.43 = (f32[2,4,1,130]{3,2,1,0:T(1,128)S(1)}, f32[2,4,1,130]{3,2,1,0:T(1,128)S(1)}, u32[]{:S(2)}, u32[]{:S(2)}) collective-permute-start(f32[2,4,1,130]{3,2,1,0:T(1,128)S(1)} %get-tuple-element.15), channel_id=1, source_target_pairs={{1,0},{2,1},{3,2},{5,4},{6,5},{7,6},{9,8},{10,9},{11,10},{13,12},{... | collective-permute-start | bytes 12488 | tf_op jit(solution)/shard_map/ppermute | solution.py:24
  207.4 4.6 %copy-start.3 = (s32[2,4]{1,0:T(2,128)S(1)}, s32[2,4]{1,0:T(2,128)}, u32[]{:S(2)}) copy-start(s32[2,4]{1,0:T(2,128)} %param.8) | copy-start | bytes 100
  207.5 5.9 %collective-permute-start.42 = (f32[2,4,1,130]{3,2,1,0:T(1,128)S(1)}, f32[2,4,1,130]{3,2,1,0:T(1,128)S(1)}, u32[]{:S(2)}, u32[]{:S(2)}) collective-permute-start(f32[2,4,1,130]{3,2,1,0:T(1,128)S(1)} %get-tuple-element.14), channel_id=1, source_target_pairs={{0,1},{1,2},{2,3},{4,5},{5,6},{6,7},{8,9},{9,10},{10,11},{12,13},{... | collective-permute-start | bytes 12488 | tf_op jit(solution)/shard_map/ppermute | solution.py:21
  216.5 99.6 %all-reduce.3.cloned.1.call-start = ((), (), s32[]{:S(2)}) async-start(), calls=%async_computation.2 | async-start | bytes 2097152
  259.6 2.9 collective-permute-start.45
  261.2 4.6 %collective-permute-start.44 = (f32[4,64,1]{2,1,0:T(8,128)S(1)}, f32[4,64,1]{2,1,0:T(8,128)S(1)}, u32[]{:S(2)}, u32[]{:S(2)}) collective-permute-start(f32[4,64,1]{2,1,0:T(8,128)S(1)} %get-tuple-element.73), channel_id=1, source_target_pairs={{4,0},{8,4},{12,8},{16,12},{20,16},{24,20},{28,24},{5,1},{9,5},{13... | collective-permute-start | bytes 3080 | tf_op jit(solution)/shard_map/ppermute | solution.py:24
  265.9 4.5 %collective-permute-start.47 = (f32[4,1,130]{2,1,0:T(1,128)S(1)}, f32[4,1,130]{2,1,0:T(1,128)S(1)}, u32[]{:S(2)}, u32[]{:S(2)}) collective-permute-start(f32[4,1,130]{2,1,0:T(1,128)S(1)} %get-tuple-element.49), channel_id=1, source_target_pairs={{0,1},{1,2},{2,3},{4,5},{5,6},{6,7},{8,9},{9,10},{10,11},{12,13},{... | collective-permute-start | bytes 6248 | tf_op jit(solution)/shard_map/ppermute | solution.py:21
  267.3 5.7 %collective-permute-start.46 = (f32[4,1,130]{2,1,0:T(1,128)S(1)}, f32[4,1,130]{2,1,0:T(1,128)S(1)}, u32[]{:S(2)}, u32[]{:S(2)}) collective-permute-start(f32[4,1,130]{2,1,0:T(1,128)S(1)} %get-tuple-element.48), channel_id=1, source_target_pairs={{1,0},{2,1},{3,2},{5,4},{6,5},{7,6},{9,8},{10,9},{11,10},{13,12},{... | collective-permute-start | bytes 6248 | tf_op jit(solution)/shard_map/ppermute | solution.py:24
  268.6 0.7 copy-start.6
Sparse Core Ops, SparseCore 0:
  216.6 38.4 reduce-scatter.1
  259.6 56.4 all-reduce.2
where the time goes:
time: 326 us; the launch traced here: 325 us
  waiting for transfers between devices  146 us (45%)
  starting transfers between devices  142 us (44%)
  between operations  15.7 us (5%)
  other arithmetic  8.29 us (3%)
  local copies, waits for them, and re-layouts  6.93 us (2%)
  matrix products  5.59 us (2%)
    ppermute x24, starting transfers between devices, padded_2(): lax.ppermute(lax.slice_in_dim(block, block.shape[dim] - width, None, axis...  111 us
    ppermute x24, waiting for transfers between devices, padded_2(): lax.ppermute(lax.slice_in_dim(block, 0, width, axis=dim), axis, backward)  52 us
    unnamed x3, waiting for transfers between devices  42.2 us
    reduce_scatter x1, waiting for transfers between devices, on_device(): lax.psum_scatter(jnp.einsum('yk,ayx->kax', part, masked, precision=lax.Pr...  38.4 us
    ppermute x24, starting transfers between devices, padded_2(): lax.ppermute(lax.slice_in_dim(block, 0, width, axis=dim), axis, backward)  31 us
    ppermute x24, waiting for transfers between devices, padded_2(): lax.ppermute(lax.slice_in_dim(block, block.shape[dim] - width, None, axis...  13.2 us
  transfers between devices with their start and end apart: 50, of which 25 were waited for; matrix products, arithmetic and copies ran while one was open for 1% of the time, Pallas kernels for 0%

commit v1 on v0

v1 whole, which is shorter than its diff:
```python
import functools
import math

import jax
import jax.numpy as jnp
import ml_dtypes
import numpy as np
from jax import lax
from jax.experimental import pallas as pl
from jax.experimental.pallas import tpu as pltpu
from jax.sharding import PartitionSpec as P

STEPS = 6
KX = 512
KY = 512
ADJ = 4
PAIRS = ADJ // 2
HALO = 16
SLOTS = 128 // HALO

MESH = pl.DeviceIdType.MESH
FLOAT = jnp.float32
HALF = jnp.bfloat16


def basis(total, modes):
    cells = np.arange(total, dtype=np.int64)
    order = np.arange(modes, dtype=np.int64)
    half = modes // 2
    wave = np.where(order < half, order, order - half + 1)
    phase = (cells[:, None] * wave[None, :] % total).astype(np.float64) * (2.0 * math.pi / total)
    return np.where(order[None, :] < half, np.cos(phase), np.sin(phase))


def halves(table):
    high = table.astype(ml_dtypes.bfloat16)
    low = (table - high.astype(np.float64)).astype(ml_dtypes.bfloat16)
    return high, low


def lon_table(total, count):
    table = basis(total, KX).T.reshape(KX, count, total // count).transpose(1, 0, 2)
    return np.stack(halves(table), axis=1)


def lat_table(total, count, scale):
    rows, own = total // count, KY // count
    table = (scale * basis(total, KY)).reshape(count, rows, count, own).transpose(2, 0, 1, 3)
    wide = np.zeros((count, count, 2, rows, 2, own))
    for member in range(2):
        wide[:, :, member, :, member] = table
    return np.stack(halves(wide.reshape(count, count * 2 * rows, 2 * own)), axis=1)


def split(x):
    high = x.astype(HALF)
    return high, (x - high.astype(FLOAT)).astype(HALF)


def turn(x, shift, axis):
    shift %= x.shape[axis]
    return x if shift == 0 else pltpu.roll(x, shift, axis)


def kernel(
    lon_count, lat_count,
    state, depth, source, gauge_lat, gauge_lon, misfit, lon_hbm, lat_hbm,
    fields, modes,
    ext, ext_depth, coef, gauges, pack_w, pack_e, got_e, got_w, lon_tab, lat_tab,
    part, pieces, gathered,
    halo_send, halo_recv, tab_sem, rs_send, rs_recv, ga_send, ga_recv,
):
    rows, cols = depth.shape
    high, wide = rows + 2 * HALO, 2 * cols
    own = modes.shape[1]
    lanes_out = modes.shape[2]
    lon = lax.axis_index("lon")
    lat = lax.axis_index("lat")
    has_e, has_w = lon < lon_count - 1, lon > 0
    has_n, has_s = lat < lat_count - 1, lat > 0

    tables = [
        pltpu.make_async_copy(lon_hbm.at[lon], lon_tab, tab_sem.at[0]),
        pltpu.make_async_copy(lat_hbm.at[lat], lat_tab, tab_sem.at[1]),
    ]
    for copy in tables:
        copy.start()

    corners = [
        (jnp.logical_and(has_e, has_n), 1, 1),
        (jnp.logical_and(has_e, has_s), 1, -1),
        (jnp.logical_and(has_w, has_n), -1, 1),
        (jnp.logical_and(has_w, has_s), -1, -1),
    ]
    barrier = pltpu.get_barrier_semaphore()
    for d in range(1, lon_count):
        pl.semaphore_signal(barrier, 1, device_id=(lax.rem(lon + d, lon_count), lat), device_id_type=MESH)
    for d in range(1, lat_count):
        pl.semaphore_signal(barrier, 1, device_id=(lon, lax.rem(lat + d, lat_count)), device_id_type=MESH)
    for there, dx, dy in corners:
        @pl.when(there)
        def _():
            pl.semaphore_signal(barrier, 1, device_id=(lon + dx, lat + dy), device_id_type=MESH)

    lane = lax.broadcasted_iota(jnp.int32, (rows, 128), 1)
    arrays = [state[f, a] for f in range(3) for a in range(ADJ)] + [depth[...]]
    for tile in range(2):
        west = jnp.zeros((rows, 128), FLOAT)
        east = west
        for slot in range(SLOTS):
            index = tile * SLOTS + slot
            if index < len(arrays):
                at = slot * HALO
                here = jnp.logical_and(lane >= at, lane < at + HALO)
                west = jnp.where(here, turn(arrays[index], at, 1), west)
                east = jnp.where(here, turn(arrays[index], at + HALO - cols, 1), east)
        pack_w[:, tile * 128:(tile + 1) * 128] = west
        pack_e[:, tile * 128:(tile + 1) * 128] = east

    diagonal = sum(there.astype(jnp.int32) for there, _, _ in corners)
    pl.semaphore_wait(barrier, lon_count - 1 + lat_count - 1 + diagonal)

    low = slice(0, HALO)
    top = slice(rows - HALO, rows)
    north = slice(rows, rows + HALO)
    south = slice(rows + HALO, high)
    every = slice(0, rows)
    plan = [
        (has_e, has_w, pack_e, got_w.at[every], 1, 0),
        (has_w, has_e, pack_w, got_e.at[every], -1, 0),
        (has_n, has_s, state.at[:, :, top], ext.at[:, :, south, 0:cols], 0, 1),
        (has_s, has_n, state.at[:, :, low], ext.at[:, :, north, 0:cols], 0, -1),
        (has_n, has_s, depth.at[top], ext_depth.at[south, 0:cols], 0, 1),
        (has_s, has_n, depth.at[low], ext_depth.at[north, 0:cols], 0, -1),
        (corners[0][0], corners[3][0], pack_e.at[top], got_w.at[south], 1, 1),
        (corners[1][0], corners[2][0], pack_e.at[low], got_w.at[north], 1, -1),
        (corners[2][0], corners[1][0], pack_w.at[top], got_e.at[south], -1, 1),
        (corners[3][0], corners[0][0], pack_w.at[low], got_e.at[north], -1, -1),
    ]

    def halo_copy(index):
        _, _, source_ref, target, dx, dy = plan[index]
        return pltpu.make_async_remote_copy(
            src_ref=source_ref, dst_ref=target,
            send_sem=halo_send.at[index], recv_sem=halo_recv.at[index],
            device_id=(lon + dx, lat + dy), device_id_type=MESH,
        )

    for index, (sends, gets, _, target, _, _) in enumerate(plan):
        @pl.when(sends)
        def _():
            halo_copy(index).start()

        @pl.when(jnp.logical_not(gets))
        def _():
            target[...] = jnp.zeros(target.shape, FLOAT)

    ext[:, :, 0:rows, 0:cols] = state[...]
    ext_depth[0:rows, 0:cols] = depth[...]
    row = lax.broadcasted_iota(jnp.int32, (high, wide), 0)
    col = lax.broadcasted_iota(jnp.int32, (high, wide), 1)
    row = lat * rows + jnp.where(row < rows + HALO, row, row - high)
    real = jnp.logical_or(col < cols + HALO, col >= wide - HALO)
    col = lon * cols + jnp.where(col < cols + HALO, col, col - wide)
    inside = (row >= 0) & (row < lat_count * rows) & (col >= 0) & (col < lon_count * cols) & real
    coef[0] = jnp.where(inside, 0.25, 0.0).astype(FLOAT)
    for a in range(ADJ):
        hit = (row == gauge_lat[a]) & (col == gauge_lon[a]) & real
        gauges[a] = jnp.where(hit, 1.0, 0.0).astype(FLOAT)
    line = lax.broadcasted_iota(jnp.int32, (rows, cols), 0)
    place = lax.broadcasted_iota(jnp.int32, (rows, cols), 1)
    mask = jnp.zeros((rows, cols), FLOAT)
    side = rows // source.shape[0]
    for i in range(source.shape[0]):
        for j in range(source.shape[1]):
            tile = (line >= i * side) & (line < (i + 1) * side) & (place >= j * side) & (place < (j + 1) * side)
            mask = jnp.where(tile, source[i, j].astype(FLOAT), mask)

    for index, (_, gets, _, _, _, _) in enumerate(plan):
        @pl.when(gets)
        def _():
            halo_copy(index).wait_recv()

    lane = lax.broadcasted_iota(jnp.int32, (high, 128), 1)

    def unpacked(index):
        tile, at = index // SLOTS, index % SLOTS * HALO
        span = slice(tile * 128, (tile + 1) * 128)
        right = turn(got_e[:, span], -at, 1)
        left = turn(got_w[:, span], -at - HALO, 1)
        return jnp.where(lane < HALO, right, jnp.where(lane >= 128 - HALO, left, 0.0))

    ext_depth[:, cols:wide] = unpacked(3 * ADJ)
    quarter = 0.25 * ext_depth[...]
    coef[1] = turn(quarter, -1, 1)
    coef[2] = turn(quarter, -1, 0)

    def rs_copy(p, d):
        target = lax.rem(lon + d, lon_count)
        return pltpu.make_async_remote_copy(
            src_ref=part.at[p, pl.ds(pl.multiple_of(target * own, own), own)],
            dst_ref=pieces.at[p, d - 1],
            send_sem=rs_send.at[p, d - 1], recv_sem=rs_recv.at[p, d - 1],
            device_id=(target, lat), device_id_type=MESH,
        )

    def ga_copy(p, d):
        return pltpu.make_async_remote_copy(
            src_ref=gathered.at[p, lat], dst_ref=gathered.at[p, lat],
            send_sem=ga_send.at[p, d - 1], recv_sem=ga_recv.at[p, d - 1],
            device_id=(lon, lax.rem(lat + d, lat_count)), device_id_type=MESH,
        )

    def ga_arrival(p, d):
        origin = lax.rem(lat + lat_count - d, lat_count)
        return pltpu.make_async_remote_copy(
            src_ref=gathered.at[p, origin], dst_ref=gathered.at[p, origin],
            send_sem=ga_send.at[p, d - 1], recv_sem=ga_recv.at[p, d - 1],
            device_id=(lon, origin), device_id_type=MESH,
        )

    for p in range(PAIRS):
        members = (2 * p, 2 * p + 1)
        for a in members:
            ext[0, a, :, cols:wide] = unpacked(a)
            ext[1, a, :, cols:wide] = unpacked(ADJ + a)
            ext[2, a, :, cols:wide] = unpacked(2 * ADJ + a)
            ext[1, a] = turn(ext[1, a], -1, 1)
            ext[2, a] = turn(ext[2, a], -1, 0)

        def step(t, carry):
            for a in members:
                east, north_ = ext[1, a], ext[2, a]
                change = (east - turn(east, 2, 1)) + (north_ - turn(north_, 2, 0))
                height = ext[0, a] + coef[0] * change + gauges[a] * misfit[t, a]
                ext[0, a] = height
                ext[1, a] = east + coef[1] * (turn(height, -2, 1) - height)
                ext[2, a] = north_ + coef[2] * (turn(height, -2, 0) - height)
            return carry

        lax.fori_loop(0, STEPS, step, 0)
        if p == 0:
            for copy in tables:
                copy.wait()
        masked = []
        for a in members:
            height = ext[0, a, 0:rows, 0:cols]
            masked.append(height * mask)
        high_m, low_m = split(jnp.concatenate(masked, axis=0))
        dims = (((1,), (1,)), ((), ()))
        part[p] = (
            lax.dot_general(lon_tab[0], high_m, dims, preferred_element_type=FLOAT)
            + lax.dot_general(lon_tab[0], low_m, dims, preferred_element_type=FLOAT)
            + lax.dot_general(lon_tab[1], high_m, dims, preferred_element_type=FLOAT)
        )
        for d in range(1, lon_count):
            rs_copy(p, d).start()
        for a in members:
            fields[0, a] = ext[0, a, 0:rows, 0:cols]
            fields[1, a] = turn(ext[1, a], 1, 1)[0:rows, 0:cols]
            fields[2, a] = turn(ext[2, a], 1, 0)[0:rows, 0:cols]

    for p in range(PAIRS):
        total = part[p, pl.ds(pl.multiple_of(lon * own, own), own)]
        for d in range(1, lon_count):
            rs_copy(p, d).wait_recv()
            total = total + pieces[p, d - 1]
        gathered[p, lat] = total
        for d in range(1, lat_count):
            ga_copy(p, d).start()

    for p in range(PAIRS):
        for d in range(1, lat_count):
            ga_arrival(p, d).wait_recv()
        high_g, low_g = split(jnp.concatenate([gathered[p, z] for z in range(lat_count)], axis=1))
        result = (
            jnp.dot(high_g, lat_tab[0], preferred_element_type=FLOAT)
            + jnp.dot(low_g, lat_tab[0], preferred_element_type=FLOAT)
            + jnp.dot(high_g, lat_tab[1], preferred_element_type=FLOAT)
        )
        for member in range(2):
            modes[2 * p + member] = result[:, member * lanes_out:(member + 1) * lanes_out]

    for index, (sends, _, _, _, _, _) in enumerate(plan):
        @pl.when(sends)
        def _():
            halo_copy(index).wait_send()
    for p in range(PAIRS):
        for d in range(1, lon_count):
            rs_copy(p, d).wait_send()
        for d in range(1, lat_count):
            ga_copy(p, d).wait_send()


def on_device(lon_count, lat_count, tables, state, depth, source_mask, gauge_lat, gauge_lon, misfit):
    rows, cols = depth.shape
    own_x, own_y = KX // lon_count, KY // lat_count
    high, wide = rows + 2 * HALO, 2 * cols
    vmem = pl.BlockSpec(memory_space=pltpu.VMEM)
    smem = pl.BlockSpec(memory_space=pltpu.SMEM)
    anywhere = pl.BlockSpec(memory_space=pl.ANY)
    dma = pltpu.SemaphoreType.DMA
    return pl.pallas_call(
        functools.partial(kernel, lon_count, lat_count),
        out_shape=(
            jax.ShapeDtypeStruct((3, ADJ, rows, cols), FLOAT),
            jax.ShapeDtypeStruct((ADJ, own_x, own_y), FLOAT),
        ),
        in_specs=[vmem, vmem, smem, smem, smem, smem, anywhere, anywhere],
        out_specs=(vmem, vmem),
        scratch_shapes=[
            pltpu.VMEM((3, ADJ, high, wide), FLOAT),
            pltpu.VMEM((high, wide), FLOAT),
            pltpu.VMEM((3, high, wide), FLOAT),
            pltpu.VMEM((ADJ, high, wide), FLOAT),
            pltpu.VMEM((rows, 256), FLOAT),
            pltpu.VMEM((rows, 256), FLOAT),
            pltpu.VMEM((high, 256), FLOAT),
            pltpu.VMEM((high, 256), FLOAT),
            pltpu.VMEM((2, KX, cols), HALF),
            pltpu.VMEM((2, lat_count * 2 * rows, 2 * own_y), HALF),
            pltpu.VMEM((PAIRS, KX, 2 * rows), FLOAT),
            pltpu.VMEM((PAIRS, lon_count - 1, own_x, 2 * rows), FLOAT),
            pltpu.VMEM((PAIRS, lat_count, own_x, 2 * rows), FLOAT),
            dma((10,)),
            dma((10,)),
            dma((2,)),
            dma((PAIRS, lon_count - 1)),
            dma((PAIRS, lon_count - 1)),
            dma((PAIRS, lat_count - 1)),
            dma((PAIRS, lat_count - 1)),
        ],
        compiler_params=pltpu.CompilerParams(
            collective_id=0, has_side_effects=True, vmem_limit_bytes=32 * 1024 * 1024
        ),
    )(state, depth, source_mask, gauge_lat, gauge_lon, misfit, *tables)


def solution(mesh):
    lon_count, lat_count = mesh.shape["lon"], mesh.shape["lat"]
    placed = (P(None, None, "lat", "lon"), P("lat", "lon"), P("lat", "lon"), P(), P(), P())

    def whole(state, depth, source_mask, gauge_lat, gauge_lon, misfit):
        total_rows, total_cols = depth.shape
        scale = 2.0 / math.sqrt(total_rows * total_cols)
        tables = (lon_table(total_cols, lon_count), lat_table(total_rows, lat_count, scale))

        def local(*args):
            constants = tuple(jnp.asarray(table) for table in tables)
            return on_device(lon_count, lat_count, constants, *args)

        return jax.shard_map(
            local,
            mesh=mesh,
            in_specs=placed,
            out_specs=(P(None, None, "lat", "lon"), P(None, "lon", "lat")),
            check_vma=False,
        )(state, depth, source_mask, gauge_lat, gauge_lon, misfit)

    return whole
```

time: 326 us -> 36.8 us (0.11)
  waiting for transfers between devices: 146 us -> 0 us
  starting transfers between devices: 142 us -> 0 us
  Pallas kernels: 0 us -> 26.8 us
  between operations: 15.7 us -> 0.65 us
  other arithmetic: 8.29 us -> 0 us
  matrix products: 5.59 us -> 0 us
    ppermute x48 -> x0, starting transfers between devices: 142 us -> none  [the longest x24 111 us: padded_2(): lax.ppermute(lax.slice_in_dim(block, block.shape[dim] - width, None, axis...]
    ppermute x48 -> x0, waiting for transfers between devices: 65.2 us -> none  [the longest x24 52 us: padded_2(): lax.ppermute(lax.slice_in_dim(block, 0, width, axis=dim), axis, backward)]
    unnamed x3 -> x0, waiting for transfers between devices: 42.2 us -> none
    reduce_scatter x1 -> x0, waiting for transfers between devices: 38.4 us -> none  [on_device(): lax.psum_scatter(jnp.einsum('yk,ayx->kax', part, masked, precision=lax.Pr...]
    pallas_call x0 -> x1, Pallas kernels: none -> 26.8 us  [on_device(): pl.pallas_call(functools.partial(kernel, lon_count, lat_count), out_shape...]
    unnamed x16 -> x17, local copies, waits for them, and re-layouts: 3.14 us -> 9.09 us
    dot_general x2 -> x0, matrix products: 5.59 us -> none  [the longest x1 3.02 us: on_device(): jnp.einsum('xk,jax->kaj', part, by_lat, precision=lax.Precision.HIGHEST)]
  transfers between devices with their start and end apart: 50 -> 0, of which waited for: 25 -> 0; matrix products, arithmetic and copies ran while one was open for 1% -> 0% of each run, Pallas kernels for 0% -> 0%
where the time goes in v1:
time: 36.8 us; the launch traced here: 36.5 us
  Pallas kernels  26.8 us (73%)
  local copies, waits for them, and re-layouts  9.09 us (25%)
  between operations  0.65 us (2%)
    pallas_call x1, Pallas kernels, on_device(): pl.pallas_call(functools.partial(kernel, lon_count, lat_count), out_shape...  26.8 us
    unnamed x17, local copies, waits for them, and re-layouts  9.09 us

profile of v1, /device:TPU:0, one launch (start us, length us, event | category | flops | bytes accessed | tf_op | source)
XLA Modules:
  0.0 36.5 jit_solution(10587335542829775897)
XLA Ops:
  0.6 0.8 %copy.10.misfit = f32[6,4]{1,0:T(8,128)S(1)} copy(f32[6,4]{0,1:T(4,128)} %param.13) | data formatting | bytes 192 | tf_op args[5]
  1.4 0.0 copy-start
  1.4 1.6 %copy-done = bf16[4,2,512,256]{3,2,1,0:T(8,128)(2,1)S(1)} copy-done((bf16[4,2,512,256]{3,2,1,0:T(8,128)(2,1)S(1)}, bf16[4,2,512,256]{3,2,1,0:T(8,128)(2,1)}, u32[]{:S(2)}) %copy-start) | copy-done | bytes 2097176
  3.0 0.0 copy-start.1
  3.0 1.6 %copy-done.1 = bf16[8,2,512,128]{3,2,1,0:T(8,128)(2,1)S(1)} copy-done((bf16[8,2,512,128]{3,2,1,0:T(8,128)(2,1)S(1)}, bf16[8,2,512,128]{3,2,1,0:T(8,128)(2,1)}, u32[]{:S(2)}) %copy-start.1) | copy-done | bytes 2097176
  4.6 0.0 copy-start.2
  4.6 1.0 %copy-done.2 = f32[3,4,64,128]{3,2,1,0:T(8,128)S(1)} copy-done((f32[3,4,64,128]{3,2,1,0:T(8,128)S(1)}, f32[3,4,64,128]{3,2,1,0:T(8,128)}, u32[]{:S(2)}) %copy-start.2) | copy-done | bytes 393240
  5.6 0.0 copy-start.3
  5.6 0.8 %copy-done.3 = f32[64,128]{1,0:T(8,128)S(1)} copy-done((f32[64,128]{1,0:T(8,128)S(1)}, f32[64,128]{1,0:T(8,128)}, u32[]{:S(2)}) %copy-start.3) | copy-done | bytes 32792
  6.3 0.0 copy-start.4
  6.3 0.7 %copy-done.4 = s32[2,4]{1,0:T(2,128)S(1)} copy-done((s32[2,4]{1,0:T(2,128)S(1)}, s32[2,4]{1,0:T(2,128)}, u32[]{:S(2)}) %copy-start.4) | copy-done | bytes 56
  7.0 0.0 copy-start.5
  7.0 0.7 %copy-done.5 = s32[4]{0:T(128)S(1)} copy-done((s32[4]{0:T(128)S(1)}, s32[4]{0:T(128)}, u32[]{:S(2)}) %copy-start.5) | copy-done | bytes 40
  7.7 0.0 copy-start.6
  7.7 0.7 %copy-done.6 = s32[4]{0:T(128)S(1)} copy-done((s32[4]{0:T(128)S(1)}, s32[4]{0:T(128)}, u32[]{:S(2)}) %copy-start.6) | copy-done | bytes 40
  8.3 26.8 %shard_map.95 = (f32[3,4,64,128]{3,2,1,0:T(8,128)S(1)}, f32[4,64,128]{2,1,0:T(8,128)S(1)}) custom-call(f32[3,4,64,128]{3,2,1,0:T(8,128)S(1)} %copy-done.2, f32[64,128]{1,0:T(8,128)S(1)} %copy-done.3, s32[2,4]{1,0:T(2,128)S(1)} %copy-done.4, s32[4]{0:T(128)S(1)} %copy-done.5, s32[4]{0:T(128)S(1)} %copy-done.6, f32[6,4]{1,0:T(8,128)S(1)} %copy.10.misfit, ...), custom_call_target="tpu_custom_call" | custom-call | tf_op jit(solution)/shard_map/pallas_call | solution.py:303
  35.1 0.7 %copy.13 = f32[3,4,64,128]{3,2,1,0:T(8,128)} copy(f32[3,4,64,128]{3,2,1,0:T(8,128)S(1)} %get-tuple-element.4) | data formatting | bytes 786432
  35.8 0.7 %copy.14 = f32[4,64,128]{2,1,0:T(8,128)} copy(f32[4,64,128]{2,1,0:T(8,128)S(1)} %get-tuple-element.5) | data formatting | bytes 262144
Async XLA Ops:
  1.4 1.6 %copy-start = (bf16[4,2,512,256]{3,2,1,0:T(8,128)(2,1)S(1)}, bf16[4,2,512,256]{3,2,1,0:T(8,128)(2,1)}, u32[]{:S(2)}) copy-start(bf16[4,2,512,256]{3,2,1,0:T(8,128)(2,1)} %constant.5.clone.lat_hbm) | copy-start | bytes 6291460
  3.0 1.6 %copy-start.1 = (bf16[8,2,512,128]{3,2,1,0:T(8,128)(2,1)S(1)}, bf16[8,2,512,128]{3,2,1,0:T(8,128)(2,1)}, u32[]{:S(2)}) copy-start(bf16[8,2,512,128]{3,2,1,0:T(8,128)(2,1)} %constant.4.clone.lon_hbm) | copy-start | bytes 6291460
  4.6 1.0 %copy-start.2 = (f32[3,4,64,128]{3,2,1,0:T(8,128)S(1)}, f32[3,4,64,128]{3,2,1,0:T(8,128)}, u32[]{:S(2)}) copy-start(f32[3,4,64,128]{3,2,1,0:T(8,128)} %state.1) | copy-start | bytes 1179652
  5.6 0.8 %copy-start.3 = (f32[64,128]{1,0:T(8,128)S(1)}, f32[64,128]{1,0:T(8,128)}, u32[]{:S(2)}) copy-start(f32[64,128]{1,0:T(8,128)} %depth.1) | copy-start | bytes 98308
  6.3 0.7 %copy-start.4 = (s32[2,4]{1,0:T(2,128)S(1)}, s32[2,4]{1,0:T(2,128)}, u32[]{:S(2)}) copy-start(s32[2,4]{1,0:T(2,128)} %source.1) | copy-start | bytes 100
  7.0 0.7 %copy-start.5 = (s32[4]{0:T(128)S(1)}, s32[4]{0:T(128)}, u32[]{:S(2)}) copy-start(s32[4]{0:T(128)} %gauge_lat.1) | copy-start | bytes 52
  7.7 0.7 %copy-start.6 = (s32[4]{0:T(128)S(1)}, s32[4]{0:T(128)}, u32[]{:S(2)}) copy-start(s32[4]{0:T(128)} %gauge_lon.1) | copy-start | bytes 52

commit v2 on v1

v2 whole, which is shorter than its diff:
```python
import functools
import math

import jax
import jax.numpy as jnp
import ml_dtypes
import numpy as np
from jax import lax
from jax.experimental import pallas as pl
from jax.experimental.pallas import tpu as pltpu
from jax.sharding import PartitionSpec as P

STEPS = 6
KX = 512
KY = 512
ADJ = 4
PAIRS = ADJ // 2
HALO = 16
SLOTS = 128 // HALO

MESH = pl.DeviceIdType.MESH
FLOAT = jnp.float32
HALF = jnp.bfloat16


def basis(total, modes):
    cells = np.arange(total, dtype=np.int64)
    order = np.arange(modes, dtype=np.int64)
    half = modes // 2
    wave = np.where(order < half, order, order - half + 1)
    phase = (cells[:, None] * wave[None, :] % total).astype(np.float64) * (2.0 * math.pi / total)
    return np.where(order[None, :] < half, np.cos(phase), np.sin(phase))


def halves(table):
    high = table.astype(ml_dtypes.bfloat16)
    low = (table - high.astype(np.float64)).astype(ml_dtypes.bfloat16)
    return high, low


def lon_table(total, count):
    chips, own = count // 2, KX // count
    table = basis(total, KX).T.reshape(chips, 2, own, chips, total // chips).transpose(3, 1, 0, 2, 4)
    return np.stack(halves(table.reshape(count, KX // 2, total // chips)), axis=1)


def lat_table(total, count, scale):
    table = (scale * basis(total, KY)).reshape(total, count, KY // count).transpose(1, 0, 2)
    return np.stack(halves(table), axis=1)


def split(x):
    high = x.astype(HALF)
    return high, (x - high.astype(FLOAT)).astype(HALF)


def turn(x, shift, axis):
    shift %= x.shape[axis]
    return x if shift == 0 else pltpu.roll(x, shift, axis)


def kernel(
    lon_count, lat_count,
    state_hbm, depth_hbm, source_hbm, gauge_lat_hbm, gauge_lon_hbm, misfit_hbm, lon_hbm, lat_hbm,
    fields, modes,
    source, gauge_lat, gauge_lon, misfit,
    ext, ext_depth, coef, gauges, pack_w, pack_e, got_e, got_w, lon_tab, lat_tab,
    shared, part, pieces, gathered,
    halo_send, halo_recv, in_sem, sh_send, sh_recv, rs_send, rs_recv, ga_send, ga_recv,
):
    rows, cols = depth_hbm.shape
    high, wide = rows + 2 * HALO, 2 * cols
    own = modes.shape[1]
    lon = lax.axis_index("lon")
    lat = lax.axis_index("lat")
    chips = lon_count // 2
    chip, core = lon // 2, lax.rem(lon, 2)
    partner = lon + 1 - 2 * core
    beside = lon - 1 + 2 * core
    has_beside = jnp.logical_and(beside >= 0, beside < lon_count)
    has_e, has_w = lon < lon_count - 1, lon > 0
    has_n, has_s = lat < lat_count - 1, lat > 0

    state = ext.at[:, :, 0:rows, 0:cols]
    depth = ext_depth.at[0:rows, 0:cols]
    pairs = [
        (state_hbm, state), (depth_hbm, depth), (source_hbm, source), (gauge_lat_hbm, gauge_lat),
        (gauge_lon_hbm, gauge_lon), (misfit_hbm, misfit), (lon_hbm.at[lon], lon_tab), (lat_hbm.at[lat], lat_tab),
    ]
    loads = [pltpu.make_async_copy(a, b, in_sem.at[i]) for i, (a, b) in enumerate(pairs)]
    for copy in loads:
        copy.start()

    corners = [
        (jnp.logical_and(has_e, has_n), 1, 1),
        (jnp.logical_and(has_e, has_s), 1, -1),
        (jnp.logical_and(has_w, has_n), -1, 1),
        (jnp.logical_and(has_w, has_s), -1, -1),
    ]
    barrier = pltpu.get_barrier_semaphore()
    pl.semaphore_signal(barrier, 1, device_id=(partner, lat), device_id_type=MESH)

    @pl.when(has_beside)
    def _():
        pl.semaphore_signal(barrier, 1, device_id=(beside, lat), device_id_type=MESH)

    for d in range(1, chips):
        target = 2 * lax.rem(chip + d, chips) + core
        pl.semaphore_signal(barrier, 1, device_id=(target, lat), device_id_type=MESH)
    for d in range(1, lat_count):
        pl.semaphore_signal(barrier, 1, device_id=(lon, lax.rem(lat + d, lat_count)), device_id_type=MESH)
    for there, dx, dy in corners:
        @pl.when(there)
        def _():
            pl.semaphore_signal(barrier, 1, device_id=(lon + dx, lat + dy), device_id_type=MESH)

    for copy in loads[2:6]:
        copy.wait()
    row = lax.broadcasted_iota(jnp.int32, (high, wide), 0)
    col = lax.broadcasted_iota(jnp.int32, (high, wide), 1)
    row = lat * rows + jnp.where(row < rows + HALO, row, row - high)
    real = jnp.logical_or(col < cols + HALO, col >= wide - HALO)
    col = lon * cols + jnp.where(col < cols + HALO, col, col - wide)
    inside = (row >= 0) & (row < lat_count * rows) & (col >= 0) & (col < lon_count * cols) & real
    coef[0] = jnp.where(inside, 0.25, 0.0).astype(FLOAT)
    for a in range(ADJ):
        hit = (row == gauge_lat[a]) & (col == gauge_lon[a]) & real
        gauges[a] = jnp.where(hit, 1.0, 0.0).astype(FLOAT)
    line = lax.broadcasted_iota(jnp.int32, (rows, cols), 0)
    place = lax.broadcasted_iota(jnp.int32, (rows, cols), 1)
    mask = jnp.zeros((rows, cols), FLOAT)
    side = rows // source.shape[0]
    for i in range(source.shape[0]):
        for j in range(source.shape[1]):
            tile = (line >= i * side) & (line < (i + 1) * side) & (place >= j * side) & (place < (j + 1) * side)
            mask = jnp.where(tile, source[i, j].astype(FLOAT), mask)

    for copy in loads[:2]:
        copy.wait()

    diagonal = sum(there.astype(jnp.int32) for there, _, _ in corners)
    pl.semaphore_wait(barrier, chips + lat_count - 1 + has_beside.astype(jnp.int32) + diagonal)

    low = slice(0, HALO)
    top = slice(rows - HALO, rows)
    north = slice(rows, rows + HALO)
    south = slice(rows + HALO, high)
    every = slice(0, rows)
    plan = [
        (has_e, has_w, pack_e, got_w.at[every], 1, 0),
        (has_w, has_e, pack_w, got_e.at[every], -1, 0),
        (has_n, has_s, ext.at[:, :, top, 0:cols], ext.at[:, :, south, 0:cols], 0, 1),
        (has_s, has_n, ext.at[:, :, low, 0:cols], ext.at[:, :, north, 0:cols], 0, -1),
        (has_n, has_s, ext_depth.at[top, 0:cols], ext_depth.at[south, 0:cols], 0, 1),
        (has_s, has_n, ext_depth.at[low, 0:cols], ext_depth.at[north, 0:cols], 0, -1),
        (corners[0][0], corners[3][0], pack_e.at[top], got_w.at[south], 1, 1),
        (corners[1][0], corners[2][0], pack_e.at[low], got_w.at[north], 1, -1),
        (corners[2][0], corners[1][0], pack_w.at[top], got_e.at[south], -1, 1),
        (corners[3][0], corners[0][0], pack_w.at[low], got_e.at[north], -1, -1),
    ]

    def halo_copy(index):
        _, _, source_ref, target, dx, dy = plan[index]
        return pltpu.make_async_remote_copy(
            src_ref=source_ref, dst_ref=target,
            send_sem=halo_send.at[index], recv_sem=halo_recv.at[index],
            device_id=(lon + dx, lat + dy), device_id_type=MESH,
        )

    def halo_start(indices):
        for index in indices:
            @pl.when(plan[index][0])
            def _():
                halo_copy(index).start()

    halo_start((2, 3, 4, 5))

    lane = lax.broadcasted_iota(jnp.int32, (rows, 128), 1)
    arrays = [ext[f, a, 0:rows, 0:cols] for f in range(3) for a in range(ADJ)] + [ext_depth[0:rows, 0:cols]]
    for tile in range(2):
        west = jnp.zeros((rows, 128), FLOAT)
        east = west
        for slot in range(SLOTS):
            index = tile * SLOTS + slot
            if index < len(arrays):
                at = slot * HALO
                here = jnp.logical_and(lane >= at, lane < at + HALO)
                west = jnp.where(here, turn(arrays[index], at, 1), west)
                east = jnp.where(here, turn(arrays[index], at + HALO - cols, 1), east)
        pack_w[:, tile * 128:(tile + 1) * 128] = west
        pack_e[:, tile * 128:(tile + 1) * 128] = east

    halo_start((6, 7, 8, 9, 0, 1))
    for _, gets, _, target, _, _ in plan:
        @pl.when(jnp.logical_not(gets))
        def _():
            target[...] = jnp.zeros(target.shape, FLOAT)

    for index, (_, gets, _, _, _, _) in enumerate(plan):
        @pl.when(gets)
        def _():
            halo_copy(index).wait_recv()

    for index in (2, 3):
        @pl.when(plan[index][0])
        def _():
            halo_copy(index).wait_send()

    lane = lax.broadcasted_iota(jnp.int32, (high, 128), 1)

    def unpacked(index):
        tile, at = index // SLOTS, index % SLOTS * HALO
        span = slice(tile * 128, (tile + 1) * 128)
        right = turn(got_e[:, span], -at, 1)
        left = turn(got_w[:, span], -at - HALO, 1)
        return jnp.where(lane < HALO, right, jnp.where(lane >= 128 - HALO, left, 0.0))

    ext_depth[:, cols:wide] = unpacked(3 * ADJ)
    quarter = 0.25 * ext_depth[...]
    coef[1] = turn(quarter, -1, 1)
    coef[2] = turn(quarter, -1, 0)

    def sh_copy(p):
        return pltpu.make_async_remote_copy(
            src_ref=shared.at[p, core], dst_ref=shared.at[p, core],
            send_sem=sh_send.at[p], recv_sem=sh_recv.at[p],
            device_id=(partner, lat), device_id_type=MESH,
        )

    def sh_arrival(p):
        return pltpu.make_async_remote_copy(
            src_ref=shared.at[p, 1 - core], dst_ref=shared.at[p, 1 - core],
            send_sem=sh_send.at[p], recv_sem=sh_recv.at[p],
            device_id=(partner, lat), device_id_type=MESH,
        )

    def rs_copy(p, d):
        target = lax.rem(chip + d, chips)
        return pltpu.make_async_remote_copy(
            src_ref=part.at[p, pl.ds(pl.multiple_of(target * own, own), own)],
            dst_ref=pieces.at[p, d - 1],
            send_sem=rs_send.at[p, d - 1], recv_sem=rs_recv.at[p, d - 1],
            device_id=(2 * target + core, lat), device_id_type=MESH,
        )

    def ga_copy(p, d):
        return pltpu.make_async_remote_copy(
            src_ref=gathered.at[p, lat], dst_ref=gathered.at[p, lat],
            send_sem=ga_send.at[p, d - 1], recv_sem=ga_recv.at[p, d - 1],
            device_id=(lon, lax.rem(lat + d, lat_count)), device_id_type=MESH,
        )

    def ga_arrival(p, d):
        origin = lax.rem(lat + lat_count - d, lat_count)
        return pltpu.make_async_remote_copy(
            src_ref=gathered.at[p, origin], dst_ref=gathered.at[p, origin],
            send_sem=ga_send.at[p, d - 1], recv_sem=ga_recv.at[p, d - 1],
            device_id=(lon, origin), device_id_type=MESH,
        )

    def prepare(p):
        for a in (2 * p, 2 * p + 1):
            ext[0, a, :, cols:wide] = unpacked(a)
            ext[1, a, :, cols:wide] = unpacked(ADJ + a)
            ext[2, a, :, cols:wide] = unpacked(2 * ADJ + a)
            ext[1, a] = turn(ext[1, a], -1, 1)
            ext[2, a] = turn(ext[2, a], -1, 0)

    def advance(p, first, last):
        def step(t, carry):
            for a in (2 * p, 2 * p + 1):
                east, north_ = ext[1, a], ext[2, a]
                change = (east - turn(east, 2, 1)) + (north_ - turn(north_, 2, 0))
                height = ext[0, a] + coef[0] * change + gauges[a] * misfit[a, t]
                ext[0, a] = height
                ext[1, a] = east + coef[1] * (turn(height, -2, 1) - height)
                ext[2, a] = north_ + coef[2] * (turn(height, -2, 0) - height)
            return carry

        lax.fori_loop(first, last, step, 0)

    def share(p):
        masked = [ext[0, a, 0:rows, 0:cols] * mask for a in (2 * p, 2 * p + 1)]
        shared[p, core] = jnp.concatenate(masked, axis=0)
        sh_copy(p).start()

    def finish(p):
        for a in (2 * p, 2 * p + 1):
            fields[0, a] = ext[0, a, 0:rows, 0:cols]
            fields[1, a] = turn(ext[1, a], 1, 1)[0:rows, 0:cols]
            fields[2, a] = turn(ext[2, a], 1, 0)[0:rows, 0:cols]

    def project(p):
        sh_arrival(p).wait_recv()
        high_m, low_m = split(jnp.concatenate([shared[p, 0], shared[p, 1]], axis=1))
        dims = (((1,), (1,)), ((), ()))
        part[p] = (
            lax.dot_general(lon_tab[0], high_m, dims, preferred_element_type=FLOAT)
            + lax.dot_general(lon_tab[0], low_m, dims, preferred_element_type=FLOAT)
            + lax.dot_general(lon_tab[1], high_m, dims, preferred_element_type=FLOAT)
        )
        for d in range(1, chips):
            rs_copy(p, d).start()

    prepare(0)
    advance(0, 0, STEPS)
    share(0)
    for copy in loads[6:]:
        copy.wait()
    prepare(1)
    advance(1, 0, STEPS // 2)
    project(0)
    advance(1, STEPS // 2, STEPS)
    share(1)
    finish(0)
    finish(1)
    project(1)

    for p in range(PAIRS):
        total = part[p, pl.ds(pl.multiple_of(chip * own, own), own)]
        for d in range(1, chips):
            rs_copy(p, d).wait_recv()
            total = total + pieces[p, d - 1]
        gathered[p, lat] = total
        for d in range(1, lat_count):
            ga_copy(p, d).start()

    blocks = [slice(z * rows, (z + 1) * rows) for z in range(lat_count) for _ in range(2)]
    by_high = jnp.concatenate([lat_tab[0, block] for block in blocks], axis=0)
    by_low = jnp.concatenate([lat_tab[1, block] for block in blocks], axis=0)
    first = lax.broadcasted_iota(jnp.int32, (own, 2 * rows), 1) < rows
    for p in range(PAIRS):
        for d in range(1, lat_count):
            ga_arrival(p, d).wait_recv()
        sums = [gathered[p, z] for z in range(lat_count)]
        high_g, low_g = split(
            jnp.concatenate(
                [
                    jnp.concatenate([jnp.where(first, x, 0.0) for x in sums], axis=1),
                    jnp.concatenate([jnp.where(first, 0.0, x) for x in sums], axis=1),
                ],
                axis=0,
            )
        )
        result = (
            jnp.dot(high_g, by_high, preferred_element_type=FLOAT)
            + jnp.dot(low_g, by_high, preferred_element_type=FLOAT)
            + jnp.dot(high_g, by_low, preferred_element_type=FLOAT)
        )
        for member in range(2):
            modes[2 * p + member] = result[member * own:(member + 1) * own]

    for index in (0, 1, 4, 5, 6, 7, 8, 9):
        @pl.when(plan[index][0])
        def _():
            halo_copy(index).wait_send()
    for p in range(PAIRS):
        sh_copy(p).wait_send()
        for d in range(1, chips):
            rs_copy(p, d).wait_send()
        for d in range(1, lat_count):
            ga_copy(p, d).wait_send()


def on_device(lon_count, lat_count, tables, state, depth, source_mask, gauge_lat, gauge_lon, misfit):
    rows, cols = depth.shape
    own_x, own_y = KX // lon_count, KY // lat_count
    high, wide = rows + 2 * HALO, 2 * cols
    vmem = pl.BlockSpec(memory_space=pltpu.VMEM)
    hbm = pl.BlockSpec(memory_space=pltpu.HBM)
    dma = pltpu.SemaphoreType.DMA
    return pl.pallas_call(
        functools.partial(kernel, lon_count, lat_count),
        out_shape=(
            jax.ShapeDtypeStruct((3, ADJ, rows, cols), FLOAT),
            jax.ShapeDtypeStruct((ADJ, own_x, own_y), FLOAT),
        ),
        in_specs=[hbm] * 8,
        out_specs=(vmem, vmem),
        scratch_shapes=[
            pltpu.SMEM(source_mask.shape, jnp.int32),
            pltpu.SMEM((ADJ,), jnp.int32),
            pltpu.SMEM((ADJ,), jnp.int32),
            pltpu.SMEM((ADJ, STEPS), FLOAT),
            pltpu.VMEM((3, ADJ, high, wide), FLOAT),
            pltpu.VMEM((high, wide), FLOAT),
            pltpu.VMEM((3, high, wide), FLOAT),
            pltpu.VMEM((ADJ, high, wide), FLOAT),
            pltpu.VMEM((rows, 256), FLOAT),
            pltpu.VMEM((rows, 256), FLOAT),
            pltpu.VMEM((high, 256), FLOAT),
            pltpu.VMEM((high, 256), FLOAT),
            pltpu.VMEM((2, KX // 2, 2 * cols), HALF),
            pltpu.VMEM((2, lat_count * rows, own_y), HALF),
            pltpu.VMEM((PAIRS, 2, 2 * rows, cols), FLOAT),
            pltpu.VMEM((PAIRS, KX // 2, 2 * rows), FLOAT),
            pltpu.VMEM((PAIRS, lon_count // 2 - 1, own_x, 2 * rows), FLOAT),
            pltpu.VMEM((PAIRS, lat_count, own_x, 2 * rows), FLOAT),
            dma((10,)),
            dma((10,)),
            dma((8,)),
            dma((PAIRS,)),
            dma((PAIRS,)),
            dma((PAIRS, lon_count // 2 - 1)),
            dma((PAIRS, lon_count // 2 - 1)),
            dma((PAIRS, lat_count - 1)),
            dma((PAIRS, lat_count - 1)),
        ],
        compiler_params=pltpu.CompilerParams(
            collective_id=0, has_side_effects=True, vmem_limit_bytes=32 * 1024 * 1024
        ),
    )(*[pltpu.with_memory_space_constraint(x, pltpu.HBM) for x in (state, depth, source_mask, gauge_lat, gauge_lon, misfit.T, *tables)])


def solution(mesh):
    lon_count, lat_count = mesh.shape["lon"], mesh.shape["lat"]
    placed = (P(None, None, "lat", "lon"), P("lat", "lon"), P("lat", "lon"), P(), P(), P())

    def whole(state, depth, source_mask, gauge_lat, gauge_lon, misfit):
        total_rows, total_cols = depth.shape
        scale = 2.0 / math.sqrt(total_rows * total_cols)
        tables = (lon_table(total_cols, lon_count), lat_table(total_rows, lat_count, scale))

        def local(*args):
            constants = tuple(jnp.asarray(table) for table in tables)
            return on_device(lon_count, lat_count, constants, *args)

        return jax.shard_map(
            local,
            mesh=mesh,
            in_specs=placed,
            out_specs=(P(None, None, "lat", "lon"), P(None, "lon", "lat")),
            check_vma=False,
        )(state, depth, source_mask, gauge_lat, gauge_lon, misfit)

    return whole
```

time: 36.8 us -> 27.8 us (0.76)
  local copies, waits for them, and re-layouts: 9.09 us -> 1.4 us
  Pallas kernels: 26.8 us -> 25.6 us
    unnamed x17 -> x2, local copies, waits for them, and re-layouts: 9.09 us -> 1.4 us
    pallas_call x1, Pallas kernels: 26.8 us -> 25.6 us  [on_device(): pl.pallas_call(functools.partial(kernel, lon_count, lat_count), out_shape...]
where the time goes in v2:
time: 27.8 us; the launch traced here: 27.6 us
  Pallas kernels  25.6 us (92%)
  local copies, waits for them, and re-layouts  1.4 us (5%)
  between operations  0.64 us (2%)
    pallas_call x1, Pallas kernels, on_device(): pl.pallas_call(functools.partial(kernel, lon_count, lat_count), out_shape...  25.6 us
    unnamed x2, local copies, waits for them, and re-layouts  1.4 us

profile of v2, /device:TPU:0, one launch (start us, length us, event | category | flops | bytes accessed | tf_op | source)
XLA Modules:
  0.0 27.6 jit_solution(4459469100319557739)
XLA Ops:
  0.6 25.6 %shard_map.95 = (f32[3,4,64,128]{3,2,1,0:T(8,128)S(1)}, f32[4,64,128]{2,1,0:T(8,128)S(1)}) custom-call(f32[3,4,64,128]{3,2,1,0:T(8,128)} %state_hbm.1, f32[64,128]{1,0:T(8,128)} %depth_hbm.1, s32[2,4]{1,0:T(2,128)} %source_hbm.1, s32[4]{0:T(128)} %gauge_lat_hbm.1, s32[4]{0:T(128)} %gauge_lon_hbm.1, f32[4,6]{1,0:T(4,128)} %bitcast.1, ...), custom_call_target="tpu_custom_call" | custom-call | tf_op jit(solution)/shard_map/pallas_call | solution.py:372
  26.2 0.7 %copy.12 = f32[3,4,64,128]{3,2,1,0:T(8,128)} copy(f32[3,4,64,128]{3,2,1,0:T(8,128)S(1)} %get-tuple-element.4) | data formatting | bytes 786432
  27.0 0.7 %copy.13 = f32[4,64,128]{2,1,0:T(8,128)} copy(f32[4,64,128]{2,1,0:T(8,128)S(1)} %get-tuple-element.5) | data formatting | bytes 262144

commit v3 on v2

--- a/solution.py
+++ b/solution.py
@@ -15,7 +15,9 @@
 KY = 512
 ADJ = 4
 PAIRS = ADJ // 2
+SPLIT = 2
 HALO = 16
+REACH = 2 * STEPS
 SLOTS = 128 // HALO
 
 MESH = pl.DeviceIdType.MESH
@@ -64,7 +66,7 @@
     state_hbm, depth_hbm, source_hbm, gauge_lat_hbm, gauge_lon_hbm, misfit_hbm, lon_hbm, lat_hbm,
     fields, modes,
     source, gauge_lat, gauge_lon, misfit,
-    ext, ext_depth, coef, gauges, pack_w, pack_e, got_e, got_w, lon_tab, lat_tab,
+    ext, ext_depth, coef, gauges, pack_w, pack_e, pack_n, pack_s, got_e, got_w, got_n, got_s, lon_tab, lat_tab,
     shared, part, pieces, gathered,
     halo_send, halo_recv, in_sem, sh_send, sh_recv, rs_send, rs_recv, ga_send, ga_recv,
 ):
@@ -149,10 +151,8 @@
     plan = [
         (has_e, has_w, pack_e, got_w.at[every], 1, 0),
         (has_w, has_e, pack_w, got_e.at[every], -1, 0),
-        (has_n, has_s, ext.at[:, :, top, 0:cols], ext.at[:, :, south, 0:cols], 0, 1),
-        (has_s, has_n, ext.at[:, :, low, 0:cols], ext.at[:, :, north, 0:cols], 0, -1),
-        (has_n, has_s, ext_depth.at[top, 0:cols], ext_depth.at[south, 0:cols], 0, 1),
-        (has_s, has_n, ext_depth.at[low, 0:cols], ext_depth.at[north, 0:cols], 0, -1),
+        (has_n, has_s, pack_n, got_s, 0, 1),
+        (has_s, has_n, pack_s, got_n, 0, -1),
         (corners[0][0], corners[3][0], pack_e.at[top], got_w.at[south], 1, 1),
         (corners[1][0], corners[2][0], pack_e.at[low], got_w.at[north], 1, -1),
         (corners[2][0], corners[1][0], pack_w.at[top], got_e.at[south], -1, 1),
@@ -173,10 +173,16 @@
             def _():
                 halo_copy(index).start()
 
-    halo_start((2, 3, 4, 5))
+    arrays = [ext.at[f, a] for f in range(3) for a in range(ADJ)] + [ext_depth]
+    for index, array in enumerate(arrays):
+        span = slice(index * REACH, (index + 1) * REACH)
+        pack_n[span] = array[rows - REACH:rows, 0:cols]
+        pack_s[span] = array[0:REACH, 0:cols]
+    for pack in (pack_n, pack_s):
+        pack[len(arrays) * REACH:] = jnp.zeros((pack.shape[0] - len(arrays) * REACH, cols), FLOAT)
+    halo_start((2, 3))
 
     lane = lax.broadcasted_iota(jnp.int32, (rows, 128), 1)
-    arrays = [ext[f, a, 0:rows, 0:cols] for f in range(3) for a in range(ADJ)] + [ext_depth[0:rows, 0:cols]]
     for tile in range(2):
         west = jnp.zeros((rows, 128), FLOAT)
         east = west
@@ -185,12 +191,12 @@
             if index < len(arrays):
                 at = slot * HALO
                 here = jnp.logical_and(lane >= at, lane < at + HALO)
-                west = jnp.where(here, turn(arrays[index], at, 1), west)
-                east = jnp.where(here, turn(arrays[index], at + HALO - cols, 1), east)
+                west = jnp.where(here, turn(arrays[index][0:rows, 0:cols], at, 1), west)
+                east = jnp.where(here, turn(arrays[index][0:rows, 0:cols], at + HALO - cols, 1), east)
         pack_w[:, tile * 128:(tile + 1) * 128] = west
         pack_e[:, tile * 128:(tile + 1) * 128] = east
 
-    halo_start((6, 7, 8, 9, 0, 1))
+    halo_start((4, 5, 6, 7, 0, 1))
     for _, gets, _, target, _, _ in plan:
         @pl.when(jnp.logical_not(gets))
         def _():
@@ -201,10 +207,11 @@
         def _():
             halo_copy(index).wait_recv()
 
-    for index in (2, 3):
-        @pl.when(plan[index][0])
-        def _():
-            halo_copy(index).wait_send()
+    for index, array in enumerate(arrays):
+        span = slice(index * REACH, (index + 1) * REACH)
+        array[rows:rows + REACH, 0:cols] = got_n[span]
+        array[rows + REACH:high - REACH, 0:cols] = jnp.zeros((high - rows - 2 * REACH, cols), FLOAT)
+        array[high - REACH:high, 0:cols] = got_s[span]
 
     lane = lax.broadcasted_iota(jnp.int32, (high, 128), 1)
 
@@ -302,21 +309,7 @@
         for d in range(1, chips):
             rs_copy(p, d).start()
 
-    prepare(0)
-    advance(0, 0, STEPS)
-    share(0)
-    for copy in loads[6:]:
-        copy.wait()
-    prepare(1)
-    advance(1, 0, STEPS // 2)
-    project(0)
-    advance(1, STEPS // 2, STEPS)
-    share(1)
-    finish(0)
-    finish(1)
-    project(1)
-
-    for p in range(PAIRS):
+    def collect(p):
         total = part[p, pl.ds(pl.multiple_of(chip * own, own), own)]
         for d in range(1, chips):
             rs_copy(p, d).wait_recv()
@@ -326,10 +319,11 @@
             ga_copy(p, d).start()
 
     blocks = [slice(z * rows, (z + 1) * rows) for z in range(lat_count) for _ in range(2)]
-    by_high = jnp.concatenate([lat_tab[0, block] for block in blocks], axis=0)
-    by_low = jnp.concatenate([lat_tab[1, block] for block in blocks], axis=0)
     first = lax.broadcasted_iota(jnp.int32, (own, 2 * rows), 1) < rows
-    for p in range(PAIRS):
+
+    def conclude(p):
+        by_high = jnp.concatenate([lat_tab[0, block] for block in blocks], axis=0)
+        by_low = jnp.concatenate([lat_tab[1, block] for block in blocks], axis=0)
         for d in range(1, lat_count):
             ga_arrival(p, d).wait_recv()
         sums = [gathered[p, z] for z in range(lat_count)]
@@ -350,7 +344,25 @@
         for member in range(2):
             modes[2 * p + member] = result[member * own:(member + 1) * own]
 
-    for index in (0, 1, 4, 5, 6, 7, 8, 9):
+    prepare(0)
+    advance(0, 0, STEPS)
+    share(0)
+    for copy in loads[6:]:
+        copy.wait()
+    prepare(1)
+    advance(1, 0, SPLIT)
+    project(0)
+    advance(1, SPLIT, STEPS)
+    share(1)
+    finish(0)
+    project(1)
+    collect(0)
+    finish(1)
+    collect(1)
+    conclude(0)
+    conclude(1)
+
+    for index in range(len(plan)):
         @pl.when(plan[index][0])
         def _():
             halo_copy(index).wait_send()
@@ -369,6 +381,7 @@
     vmem = pl.BlockSpec(memory_space=pltpu.VMEM)
     hbm = pl.BlockSpec(memory_space=pltpu.HBM)
     dma = pltpu.SemaphoreType.DMA
+    strip = ((3 * ADJ + 1) * REACH + 4, cols)
     return pl.pallas_call(
         functools.partial(kernel, lon_count, lat_count),
         out_shape=(
@@ -388,16 +401,20 @@
             pltpu.VMEM((ADJ, high, wide), FLOAT),
             pltpu.VMEM((rows, 256), FLOAT),
             pltpu.VMEM((rows, 256), FLOAT),
+            pltpu.VMEM(strip, FLOAT),
+            pltpu.VMEM(strip, FLOAT),
             pltpu.VMEM((high, 256), FLOAT),
             pltpu.VMEM((high, 256), FLOAT),
+            pltpu.VMEM(strip, FLOAT),
+            pltpu.VMEM(strip, FLOAT),
             pltpu.VMEM((2, KX // 2, 2 * cols), HALF),
             pltpu.VMEM((2, lat_count * rows, own_y), HALF),
             pltpu.VMEM((PAIRS, 2, 2 * rows, cols), FLOAT),
             pltpu.VMEM((PAIRS, KX // 2, 2 * rows), FLOAT),
             pltpu.VMEM((PAIRS, lon_count // 2 - 1, own_x, 2 * rows), FLOAT),
             pltpu.VMEM((PAIRS, lat_count, own_x, 2 * rows), FLOAT),
-            dma((10,)),
-            dma((10,)),
+            dma((8,)),
+            dma((8,)),
             dma((8,)),
             dma((PAIRS,)),
             dma((PAIRS,)),

time: 27.8 us -> 27.2 us (0.978)
  Pallas kernels: 25.6 us -> 25 us
    pallas_call x1, Pallas kernels: 25.6 us -> 25 us  [on_device(): pl.pallas_call(functools.partial(kernel, lon_count, lat_count), out_shape...]
where the time goes in v3:
time: 27.2 us; the launch traced here: 27.1 us
  Pallas kernels  25 us (92%)
  local copies, waits for them, and re-layouts  1.4 us (5%)
  between operations  0.64 us (2%)
    pallas_call x1, Pallas kernels, on_device(): pl.pallas_call(functools.partial(kernel, lon_count, lat_count), out_shape...  25 us
    unnamed x2, local copies, waits for them, and re-layouts  1.4 us

profile of v3, /device:TPU:0, one launch (start us, length us, event | category | flops | bytes accessed | tf_op | source)
XLA Modules:
  0.0 27.1 jit_solution(16086961165693953217)
XLA Ops:
  0.6 25.0 %shard_map.95 = (f32[3,4,64,128]{3,2,1,0:T(8,128)S(1)}, f32[4,64,128]{2,1,0:T(8,128)S(1)}) custom-call(f32[3,4,64,128]{3,2,1,0:T(8,128)} %state_hbm.1, f32[64,128]{1,0:T(8,128)} %depth_hbm.1, s32[2,4]{1,0:T(2,128)} %source_hbm.1, s32[4]{0:T(128)} %gauge_lat_hbm.1, s32[4]{0:T(128)} %gauge_lon_hbm.1, f32[4,6]{1,0:T(4,128)} %bitcast.1, ...), custom_call_target="tpu_custom_call" | custom-call | tf_op jit(solution)/shard_map/pallas_call | solution.py:385
  25.7 0.7 %copy.12 = f32[3,4,64,128]{3,2,1,0:T(8,128)} copy(f32[3,4,64,128]{3,2,1,0:T(8,128)S(1)} %get-tuple-element.4) | data formatting | bytes 786432
  26.4 0.7 %copy.13 = f32[4,64,128]{2,1,0:T(8,128)} copy(f32[4,64,128]{2,1,0:T(8,128)S(1)} %get-tuple-element.5) | data formatting | bytes 262144
